TPU v7x, 32 devices: a whole 2x2x4 slice. The times are simulated.
32 devices in a mesh: grp: 2 (over y), gx: 4 (over z), gy: 4 (over x, core).
Axes of the slice: x: 2, y: 2, z: 4, core: 2. Of those that a mesh axis runs over, the one named last changes fastest.
Arguments:
- source: bfloat16 [512, 256, 128], P(('grp', 'gx'), 'gy'), parts along dimension 0, may hold values from -6 to 6
- field: bfloat16 [512, 256, 128], P(('grp', 'gx'), 'gy'), parts along dimension 0, may hold values from -3 to 3
- kerr: float32 [512, 256], P(('grp', 'gx'), 'gy'), parts along dimension 0, may hold values from 0.05 to 0.3
- wave: float32 [512, 256], P(('grp', 'gx'), 'gy'), parts along dimension 0, may hold values from 0.5 to 2
- leaf_ops: bfloat16 [16, 16, 256, 256], P('gx', 'gy'), may hold values from -0.375 to 0.375
- transfer_ops: float32 [4, 256, 64], P('gx', 'gy'), may hold values from 0 to 1
Outputs:
- updated: bfloat16 [512, 256, 128], P(('grp', 'gx'), 'gy'), parts along dimension 0
- residual: bfloat16 [512, 256, 128], P(('grp', 'gx'), 'gy'), parts along dimension 0
There are 2 independent parts, one for each index of `grp`. A program takes and returns all parts, laid end to end along the dimension named above; an argument that names none is the same for every part. Nothing has to cross between parts.
All inputs are finite; a program needn't handle non-finite values.
Results may differ from a plain program's by a relative error of at most 0.015.
Values may be sent and summed in bfloat16 or wider, within the bound.
No kernel may reach another device: no remote copies, remote signals or barrier semaphores. Data moves between devices by JAX's collectives and lax.ppermute only.
A program may use at most 64 MiB of HBM per device.

v0:
```python
import jax
import jax.numpy as jnp
from jax import lax
from jax.sharding import PartitionSpec as P

lift_weight = 0.3


def entering(part, axis, combine, identity, reverse):
    count = lax.axis_size(axis)
    place = lax.axis_index(axis)
    ahead = count - 1 - place if reverse else place
    gathered = jax.tree.map(lambda a: lax.all_gather(a, axis), part)
    state = jax.tree.map(lambda a, e: jnp.zeros_like(a) + jnp.asarray(e, a.dtype), part, identity)

    def one(hop, state):
        source = count - 1 - hop if reverse else hop
        return combine(
            state, jax.tree.map(lambda a: lax.dynamic_index_in_dim(a, source, 0, False), gathered)
        )

    return lax.fori_loop(0, ahead, one, state)


def with_halo(block, sides, width):
    for axis, dim in sides:
        count = lax.axis_size(axis)
        forward = [(i, i + 1) for i in range(count - 1)]
        backward = [(target, source) for source, target in forward]
        low = lax.ppermute(
            lax.slice_in_dim(block, block.shape[dim] - width, None, axis=dim), axis, forward
        )
        high = lax.ppermute(lax.slice_in_dim(block, 0, width, axis=dim), axis, backward)
        block = jnp.concatenate([low, block, high], axis=dim)
    return block


def product(left, right):
    return jnp.dot(left, right, precision=lax.Precision.HIGHEST)


def compose(earlier, later):
    return (product(later[0], earlier[0]), product(later[0], earlier[1]) + later[1])


def per_device(source, field, kerr, wave, leaf_ops, transfer_ops):
    x_points, y_points, columns = source.shape
    leaves_x, leaves_y, leaf_pts, _ = leaf_ops.shape
    points = x_points // leaves_x
    source_f = source.astype(jnp.float32)
    field_f = field.astype(jnp.float32)
    kerr_source = (source_f - kerr[:, :, None] * field_f * field_f * field_f).astype(jnp.bfloat16)
    leaves = (
        kerr_source.reshape(leaves_x, points, leaves_y, points, columns)
        .transpose(0, 2, 1, 3, 4)
        .reshape(leaves_x, leaves_y, leaf_pts, columns)
    )
    solved = jnp.einsum("abpq,abqn->abpn", leaf_ops, leaves, preferred_element_type=jnp.float32)
    particular_solution = (
        solved.reshape(leaves_x, leaves_y, points, points, columns)
        .transpose(0, 2, 1, 3, 4)
        .reshape(x_points, y_points, columns)
    )
    right_face = particular_solution[-1]
    left_face = particular_solution[0]
    own_map = transfer_ops[0]
    ident = (jnp.eye(y_points, dtype=jnp.float32), jnp.zeros((y_points, columns), jnp.float32))
    _, w_in = entering((own_map, right_face), "gx", compose, ident, False)
    _, z_in = entering((own_map.T, left_face), "gx", compose, ident, True)
    offsets = jnp.arange(x_points).astype(jnp.float32)
    left_prof = ((x_points - offsets) / x_points)[:, None, None]
    right_prof = ((offsets + 1.0) / x_points)[:, None, None]
    updated = (
        particular_solution + lift_weight * (left_prof * w_in[None] + right_prof * z_in[None])
    ).astype(jnp.bfloat16)
    padded_patches = with_halo(updated, (("gx", 0), ("gy", 1)), 1).astype(jnp.float32)
    values = updated.astype(jnp.float32)
    laplacian_operator = (
        padded_patches[2:, 1:-1]
        + padded_patches[:-2, 1:-1]
        + padded_patches[1:-1, 2:]
        + padded_patches[1:-1, :-2]
        - 4.0 * values
    )
    residual = (
        laplacian_operator
        + wave[:, :, None] * values
        + kerr[:, :, None] * values * values * values
        - source_f
    )
    return (updated, residual.astype(jnp.bfloat16))


def solution(mesh):
    return jax.shard_map(
        per_device,
        mesh=mesh,
        in_specs=(
            P(("grp", "gx"), "gy", None),
            P(("grp", "gx"), "gy", None),
            P(("grp", "gx"), "gy"),
            P(("grp", "gx"), "gy"),
            P("gx", "gy", None, None),
            P("gx", "gy", None),
        ),
        out_specs=(P(("grp", "gx"), "gy", None), P(("grp", "gx"), "gy", None)),
        check_vma=False,
    )
```

profile of v0, /device:TPU:1, one launch (start us, length us, event | category | flops | bytes accessed | tf_op | source)
XLA Modules:
  0.0 92.6 jit_solution(15015385495708423856)
XLA Ops:
  0.6 0.0 copy-start
  0.7 1.0 %copy.23 = f32[1,64,64]{1,2,0:T(8,128)S(1)} copy(f32[1,64,64]{2,1,0:T(8,128)} %param.15) | data formatting | bytes 32768 | tf_op args[5]
  1.6 12.3 %all_gather.15 = f32[4,64,64]{2,1,0:T(8,128)S(1)} all-gather(f32[1,64,64]{2,1,0:T(8,128)} %param.15), channel_id=1, replica_groups=mesh['grp'=2,'gx'=4,'gy'=4] {'gx'}, dimensions={0}, use_global_device_ids=true | all-gather | bytes 81920 | tf_op jit(solution)/shard_map/all_gather | solution.py:13
  14.0 10.5 %all-gather = f32[256,64]{1,0:T(8,128)S(1)} all-gather(f32[64,64]{1,0:T(8,128)S(1)} %bitcast.47), channel_id=2, replica_groups=mesh['grp'=2,'gx'=4,'gy'=4] {'gx'}, dimensions={0}, use_global_device_ids=true | all-gather | bytes 81920 | tf_op jit(solution)/shard_map/all_gather | solution.py:13
  24.5 1.9 %fusion.6 = bf16[64,64,128]{2,1,0:T(8,128)(2,1)S(1)} fusion(bf16[64,64,128]{2,1,0:T(8,128)(2,1)} %param.10, bf16[64,64,128]{2,1,0:T(8,128)(2,1)} %param.11, f32[64,64]{1,0:T(8,128)} %param.12), kind=kLoop, calls=%fused_computation.16 | loop fusion | flops 3670016 | bytes 3162112 | tf_op jit(solution)/shard_map/convert_element_type | solution.py:52
  26.4 0.3 copy.19
  26.7 2.2 %convolution_bitcast_fusion = f32[4,4,256,128]{2,3,1,0:T(8,128)} fusion(bf16[4,4,256,128]{3,2,1,0:T(8,128)(2,1)S(1)} %bitcast.44, bf16[4,4,256,256]{3,2,1,0:T(8,128)(2,1)S(1)} %copy-done), kind=kOutput, calls=%fused_computation.25 | convolution fusion | flops 268435456 | bytes 5242880 | tf_op jit(solution)/shard_map/abpq,abqn->abpn/dot_general | solution.py:58
  28.9 2.9 %copy.21 = f32[4,4,256,128]{3,2,1,0:T(8,128)} copy(f32[4,4,256,128]{2,3,1,0:T(8,128)} %convolution_bitcast_fusion) | data formatting | bytes 4194304 | tf_op jit(solution)/shard_map/abpq,abqn->abpn/dot_general | solution.py:58
  31.8 1.8 %copy.22 = f32[4,16,4,16,128]{4,3,2,1,0:T(8,128)S(1)} copy(f32[4,16,4,16,128]{4,3,1,2,0:T(8,128)} %bitcast.43) | data formatting | bytes 4194304 | tf_op jit(solution)/shard_map/transpose | solution.py:61
  33.6 1.3 %copy-done.1 = f32[4,16,4,16,128]{4,3,2,1,0:T(8,128)} copy-done((f32[4,16,4,16,128]{4,3,2,1,0:T(8,128)}, f32[4,16,4,16,128]{4,3,2,1,0:T(8,128)S(1)}, u32[]{:S(2)}) %copy-start.1) | copy-done | bytes 2097176
  35.0 10.5 %all_gather.16 = f32[4,64,128]{2,1,0:T(8,128)S(1)} all-gather(f32[1,64,128]{2,1,0:T(8,128)S(1)} %get-tuple-element.152), channel_id=1, replica_groups=mesh['grp'=2,'gx'=4,'gy'=4] {'gx'}, dimensions={0}, use_global_device_ids=true | all-gather | bytes 163840 | tf_op jit(solution)/shard_map/all_gather | solution.py:13
  45.4 10.8 %all_gather.19 = f32[4,64,128]{2,1,0:T(8,128)S(1)} all-gather(f32[1,64,128]{2,1,0:T(8,128)S(1)} %get-tuple-element.153), channel_id=1, replica_groups=mesh['grp'=2,'gx'=4,'gy'=4] {'gx'}, dimensions={0}, use_global_device_ids=true | all-gather | bytes 163840 | tf_op jit(solution)/shard_map/all_gather | solution.py:13
  56.3 0.6 while.27
  56.3 0.2 convolution_add_fusion.5
  56.5 0.2 convolution_add_fusion.5
  56.7 0.2 convolution_add_fusion.5
  56.9 2.1 %add_convert_fusion = bf16[64,64,128]{2,1,0:T(8,128)(2,1)S(1)} fusion(f32[64,64,128]{2,1,0:T(8,128)} %bitcast.41, f32[64,128]{1,0:T(8,128)S(1)} %get-tuple-element.131, f32[64]{0:T(128)S(1)} %get-tuple-element.158, f32[64,128]{1,0:T(8,128)S(1)} %get-tuple-element.130, f32[64]{0:T(128)S(1)} %get-tuple-element.159), kind=kLoop, calls=%fused_computation.24 | loop fusion | flops 3145728 | bytes 3211776 | tf_op jit(solution)/shard_map/convert_element_type | solution.py:75
  59.0 0.0 copy-start.3
  59.0 3.1 %collective-permute-start = (bf16[1,64,128]{2,1,0:T(8,128)(2,1)S(1)}, bf16[1,64,128]{2,1,0:T(8,128)(2,1)S(1)}, u32[]{:S(2)}, u32[]{:S(2)}) collective-permute-start(bf16[1,64,128]{2,1,0:T(8,128)(2,1)S(1)} %get-tuple-element.156), channel_id=1, source_target_pairs={{0,4},{4,8},{8,12},{1,5},{5,9},{9,13},{2,6},{6,10},{10,14},{3,7},{... | collective-permute-start | bytes 49160 | tf_op jit(solution)/shard_map/ppermute | solution.py:30
  62.2 0.0 copy-start.4
  62.2 0.0 copy-start.5
  62.2 0.0 copy-start.6
  62.2 1.6 %collective-permute-start.1 = (bf16[1,64,128]{2,1,0:T(8,128)(2,1)S(1)}, bf16[1,64,128]{2,1,0:T(8,128)(2,1)S(1)}, u32[]{:S(2)}, u32[]{:S(2)}) collective-permute-start(bf16[1,64,128]{2,1,0:T(8,128)(2,1)S(1)} %get-tuple-element.157), channel_id=1, source_target_pairs={{4,0},{8,4},{12,8},{5,1},{9,5},{13,9},{6,2},{10,6},{14,10},{7,3},{... | collective-permute-start | bytes 49160 | tf_op jit(solution)/shard_map/ppermute | solution.py:33
  63.8 0.0 collective-permute-done
  63.8 3.5 %collective-permute-done.1 = bf16[1,64,128]{2,1,0:T(8,128)(2,1)S(1)} collective-permute-done((bf16[1,64,128]{2,1,0:T(8,128)(2,1)S(1)}, bf16[1,64,128]{2,1,0:T(8,128)(2,1)S(1)}, u32[]{:S(2)}, u32[]{:S(2)}) %collective-permute-start.1) | collective-permute-done | bytes 16416 | tf_op jit(solution)/shard_map/ppermute | solution.py:33
  67.2 0.1 pad_maximum_fusion.2
  67.3 16.3 %collective-permute-start.2 = (bf16[66,1,128]{2,1,0:T(2,128)(2,1)S(1)}, bf16[66,1,128]{2,1,0:T(2,128)(2,1)S(1)}, u32[]{:S(2)}, u32[]{:S(2)}) collective-permute-start(bf16[66,1,128]{2,1,0:T(2,128)(2,1)S(1)} %get-tuple-element.154), channel_id=1, source_target_pairs={{0,1},{1,2},{2,3},{4,5},{5,6},{6,7},{8,9},{9,10},{10,11},{12,13},{... | collective-permute-start | bytes 50696 | tf_op jit(solution)/shard_map/ppermute | solution.py:30
  83.6 1.9 %collective-permute-start.3 = (bf16[66,1,128]{2,1,0:T(2,128)(2,1)S(1)}, bf16[66,1,128]{2,1,0:T(2,128)(2,1)S(1)}, u32[]{:S(2)}, u32[]{:S(2)}) collective-permute-start(bf16[66,1,128]{2,1,0:T(2,128)(2,1)S(1)} %get-tuple-element.155), channel_id=1, source_target_pairs={{1,0},{2,1},{3,2},{5,4},{6,5},{7,6},{9,8},{10,9},{11,10},{13,12},{... | collective-permute-start | bytes 50696 | tf_op jit(solution)/shard_map/ppermute | solution.py:33
  85.6 0.0 collective-permute-done.2
  85.6 3.3 %collective-permute-done.3 = bf16[66,1,128]{2,1,0:T(2,128)(2,1)S(1)} collective-permute-done((bf16[66,1,128]{2,1,0:T(2,128)(2,1)S(1)}, bf16[66,1,128]{2,1,0:T(2,128)(2,1)S(1)}, u32[]{:S(2)}, u32[]{:S(2)}) %collective-permute-start.3) | collective-permute-done | bytes 16928 | tf_op jit(solution)/shard_map/ppermute | solution.py:33
  88.9 0.5 maximum_convert_fusion
  89.4 3.2 %fusion.7 = bf16[64,64,128]{2,1,0:T(8,128)(2,1)} fusion(bf16[64,64,128]{2,1,0:T(8,128)(2,1)S(1)} %copy-done.4, f32[66,66,128]{2,1,0:T(8,128)S(1)} %maximum_convert_fusion, f32[64,64]{1,0:T(8,128)S(1)} %copy-done.6, f32[64,64]{1,0:T(8,128)S(1)} %copy-done.5, f32[64,64,128]{2,1,0:T(8,128)S(1)} %bitcast.42, f32[64,128]{1,0:T(8,128)S(1)} %get-tuple-element.131, ...), kind=kLoop, calls=%fused_computation.17 | loop fusion | flops 11010048 | bytes 12681728 | tf_op jit(solution)/shard_map/convert_element_type | solution.py:91
  (17 shorter events, 0.1 us)
Async XLA Ops:
  0.6 26.1 %copy-start = (bf16[4,4,256,256]{3,2,1,0:T(8,128)(2,1)S(1)}, bf16[4,4,256,256]{3,2,1,0:T(8,128)(2,1)}, u32[]{:S(2)}) copy-start(bf16[4,4,256,256]{3,2,1,0:T(8,128)(2,1)} %param.14) | copy-start | bytes 6291460
  33.6 1.3 %copy-start.1 = (f32[4,16,4,16,128]{4,3,2,1,0:T(8,128)}, f32[4,16,4,16,128]{4,3,2,1,0:T(8,128)S(1)}, u32[]{:S(2)}) copy-start(f32[4,16,4,16,128]{4,3,2,1,0:T(8,128)S(1)} %copy.22) | copy-start | bytes 6291460
  59.0 30.4 %copy-start.3 = (bf16[64,64,128]{2,1,0:T(8,128)(2,1)}, bf16[64,64,128]{2,1,0:T(8,128)(2,1)S(1)}, u32[]{:S(2)}) copy-start(bf16[64,64,128]{2,1,0:T(8,128)(2,1)S(1)} %add_convert_fusion) | copy-start | bytes 3145732
  59.0 4.8 %collective-permute-start = (bf16[1,64,128]{2,1,0:T(8,128)(2,1)S(1)}, bf16[1,64,128]{2,1,0:T(8,128)(2,1)S(1)}, u32[]{:S(2)}, u32[]{:S(2)}) collective-permute-start(bf16[1,64,128]{2,1,0:T(8,128)(2,1)S(1)} %get-tuple-element.156), channel_id=1, source_target_pairs={{0,4},{4,8},{8,12},{1,5},{5,9},{9,13},{2,6},{6,10},{10,14},{3,7},{... | collective-permute-start | bytes 49160 | tf_op jit(solution)/shard_map/ppermute | solution.py:30
  62.2 27.2 %copy-start.2 = (f32[4,16,4,16,128]{4,3,2,1,0:T(8,128)S(1)}, f32[4,16,4,16,128]{4,3,2,1,0:T(8,128)}, u32[]{:S(2)}) copy-start(f32[4,16,4,16,128]{4,3,2,1,0:T(8,128)} %copy-done.1) | copy-start | bytes 6291460
  62.2 27.2 %copy-start.4 = (bf16[64,64,128]{2,1,0:T(8,128)(2,1)S(1)}, bf16[64,64,128]{2,1,0:T(8,128)(2,1)}, u32[]{:S(2)}) copy-start(bf16[64,64,128]{2,1,0:T(8,128)(2,1)} %param.10) | copy-start | bytes 3145732
  62.2 27.2 %copy-start.5 = (f32[64,64]{1,0:T(8,128)S(1)}, f32[64,64]{1,0:T(8,128)}, u32[]{:S(2)}) copy-start(f32[64,64]{1,0:T(8,128)} %param.12) | copy-start | bytes 49156
  62.2 27.2 %copy-start.6 = (f32[64,64]{1,0:T(8,128)S(1)}, f32[64,64]{1,0:T(8,128)}, u32[]{:S(2)}) copy-start(f32[64,64]{1,0:T(8,128)} %param.13) | copy-start | bytes 49156
  62.2 5.0 %collective-permute-start.1 = (bf16[1,64,128]{2,1,0:T(8,128)(2,1)S(1)}, bf16[1,64,128]{2,1,0:T(8,128)(2,1)S(1)}, u32[]{:S(2)}, u32[]{:S(2)}) collective-permute-start(bf16[1,64,128]{2,1,0:T(8,128)(2,1)S(1)} %get-tuple-element.157), channel_id=1, source_target_pairs={{4,0},{8,4},{12,8},{5,1},{9,5},{13,9},{6,2},{10,6},{14,10},{7,3},{... | collective-permute-start | bytes 49160 | tf_op jit(solution)/shard_map/ppermute | solution.py:33
  67.3 18.3 %collective-permute-start.2 = (bf16[66,1,128]{2,1,0:T(2,128)(2,1)S(1)}, bf16[66,1,128]{2,1,0:T(2,128)(2,1)S(1)}, u32[]{:S(2)}, u32[]{:S(2)}) collective-permute-start(bf16[66,1,128]{2,1,0:T(2,128)(2,1)S(1)} %get-tuple-element.154), channel_id=1, source_target_pairs={{0,1},{1,2},{2,3},{4,5},{5,6},{6,7},{8,9},{9,10},{10,11},{12,13},{... | collective-permute-start | bytes 50696 | tf_op jit(solution)/shard_map/ppermute | solution.py:30
  83.6 5.2 %collective-permute-start.3 = (bf16[66,1,128]{2,1,0:T(2,128)(2,1)S(1)}, bf16[66,1,128]{2,1,0:T(2,128)(2,1)S(1)}, u32[]{:S(2)}, u32[]{:S(2)}) collective-permute-start(bf16[66,1,128]{2,1,0:T(2,128)(2,1)S(1)} %get-tuple-element.155), channel_id=1, source_target_pairs={{1,0},{2,1},{3,2},{5,4},{6,5},{7,6},{9,8},{10,9},{11,10},{13,12},{... | collective-permute-start | bytes 50696 | tf_op jit(solution)/shard_map/ppermute | solution.py:33
where the time goes:
time: 93 us; the launch traced here: 92.6 us
  blocking collectives  44.1 us (47%)
  starting transfers between devices  22.9 us (25%)
  other arithmetic  7.78 us (8%)
  local copies, waits for them, and re-layouts  7.37 us (8%)
  waiting for transfers between devices  6.78 us (7%)
  matrix products  2.68 us (3%)
    all_gather x4, blocking collectives, entering(): gathered = jax.tree.map(lambda a: lax.all_gather(a, axis), part)  44.1 us
    ppermute x2, starting transfers between devices, with_halo(): lax.ppermute(lax.slice_in_dim(block, block.shape[dim] - width, None, axis...  19.5 us
    ppermute x2, waiting for transfers between devices, with_halo(): lax.ppermute(lax.slice_in_dim(block, 0, width, axis=dim), axis, backward)  6.77 us
    ppermute x2, starting transfers between devices, with_halo(): lax.ppermute(lax.slice_in_dim(block, 0, width, axis=dim), axis, backward)  3.48 us
    convert_element_type x1, other arithmetic, per_device(): return (updated, residual.astype(jnp.bfloat16))  3.22 us
    dot_general x1, local copies, waits for them, and re-layouts, per_device(): jnp.einsum('abpq,abqn->abpn', leaf_ops, leaves, preferred_element_type=jn...  2.92 us
    unnamed x15, local copies, waits for them, and re-layouts  2.34 us
    dot_general x1, matrix products, per_device(): jnp.einsum('abpq,abqn->abpn', leaf_ops, leaves, preferred_element_type=jn...  2.18 us
  transfers between devices with their start and end apart: 4, of which 2 were waited for; matrix products, arithmetic and copies ran while one was open for 0% of the time, Pallas kernels for 0%

commit v1 on v0

v1 whole, which is shorter than its diff:
```python
import functools

import jax
import jax.numpy as jnp
from jax import lax
from jax.experimental import pallas as pl
from jax.experimental.pallas import tpu as pltpu
from jax.sharding import PartitionSpec as P

lift_weight = 0.3
f32, bf16 = jnp.float32, jnp.bfloat16
VMEM = pl.BlockSpec(memory_space=pltpu.VMEM)
ANY = pl.BlockSpec(memory_space=pl.ANY)


def call(body, outs, ins, out_specs=None, scratch=(), cost=(0, 0), aliases=None):
    def run(*args):
        return pl.pallas_call(
            body,
            out_shape=outs,
            in_specs=ins,
            out_specs=out_specs if out_specs is not None else jax.tree.map(lambda _: VMEM, outs),
            scratch_shapes=scratch,
            input_output_aliases=aliases or {},
            compiler_params=pltpu.CompilerParams(vmem_limit_bytes=24 << 20),
            cost_estimate=pl.CostEstimate(
                flops=cost[0], bytes_accessed=cost[1], transcendentals=0
            ),
        )(*args)

    return run


def matmul(a, b):
    return jnp.dot(a, b, preferred_element_type=f32)


def kerr_column(source, field, kerr):
    s, f = source.astype(f32), field.astype(f32)
    return (s - kerr * f * f * f).astype(bf16)


def faces_body(
    half, points, source, field, kerr, leaf_ops, transfer, msg, edge, src, fld, ops, sems
):
    lx, ly, pts, _ = leaf_ops.shape
    xs, ys, cols = source.shape
    copies = []
    for e, (x0, a, r0) in enumerate(((0, 0, 0), (xs - points, lx - 1, pts - points))):
        group = [
            pltpu.make_async_copy(source.at[pl.ds(x0, points)], src.at[e], sems.at[e, 0]),
            pltpu.make_async_copy(field.at[pl.ds(x0, points)], fld.at[e], sems.at[e, 1]),
            pltpu.make_async_copy(
                leaf_ops.at[a, :, pl.ds(r0, points), :], ops.at[e], sems.at[e, 2]
            ),
        ]
        for c in group:
            c.start()
        copies.append(group)
    is_a = lax.axis_index("gx") < half
    own = transfer[0]
    x_map = jnp.where(is_a, own, own.T).astype(bf16)
    faces = []
    for e in range(2):
        x0 = 0 if e == 0 else xs - points
        kt = kerr[x0 : x0 + points, :].T
        for c in copies[e]:
            c.wait()
        for q in range(points):
            edge[e, q] = kerr_column(src[e, q], fld[e, q], kt[:, q : q + 1])
        rows = []
        for b in range(ly):
            rhs = edge[e, :, b * points : (b + 1) * points, :].reshape(pts, cols)
            rows.append(matmul(ops[e, b], rhs))
        faces.append(jnp.concatenate(rows, axis=0).astype(bf16))
    left, right = faces
    msg[0:ys, :] = jnp.where(is_a, right, left)
    msg[ys : 2 * ys, :] = jnp.where(is_a, left, right)
    msg[2 * ys :, :] = jnp.concatenate([x_map[: ys // 2], x_map[ys // 2 :]], axis=1)


def split_message(m, ys):
    packed = m[2 * ys :]
    return m[:ys], m[ys : 2 * ys], jnp.concatenate([packed[:, :ys], packed[:, ys:]], axis=0)


def leaves_body(points, edge, source, field, kerr, leaf_ops, part, ends, rhs_all):
    lx, ly, pts, _ = leaf_ops.shape
    xs, ys, cols = source.shape
    kt = kerr[...].T
    for a in range(lx):
        for q in range(points):
            x = a * points + q
            if a == 0:
                col = edge[0, q]
            elif a == lx - 1:
                col = edge[1, q]
            else:
                col = kerr_column(source[x], field[x], kt[:, x : x + 1])
            rhs_all[x] = col
        for b in range(ly):
            rhs = rhs_all[a * points : (a + 1) * points, b * points : (b + 1) * points, :]
            out = matmul(leaf_ops[a, b], rhs.reshape(pts, cols))
            for q in range(points):
                r = (a * points + q) * ys + b * points
                part[r : r + points, :] = out[q * points : (q + 1) * points, :]
    ends[0:xs, :] = part[pl.ds(0, xs, stride=ys), :]
    ends[xs:, :] = part[pl.ds(ys - 1, xs, stride=ys), :]


def compose_body(count, xs, own, got, msg, keep, inner_map):
    ys = own.shape[1] // 2
    place = lax.axis_index("gx")
    inner = (place == count // 2 - 1) | (place == count // 2)
    f_own, g_own, x_own = split_message(own[...], ys)
    f_got, g_got, x_got = split_message(got[...], ys)
    f_in = jnp.where(inner, f_own, f_got)
    g_in = jnp.where(inner, g_own, g_got)
    x_in = jnp.where(inner, x_own, x_got)
    f_out = jnp.where(inner, f_got, f_own)
    reach = matmul(x_in, f_out) + f_in.astype(f32)
    msg[0:ys, :] = reach.astype(bf16)
    msg[ys:, :] = (f_in.astype(f32) + (lift_weight / xs) * f_out.astype(f32)).astype(bf16)
    keep[0] = f_out.astype(f32)
    keep[1] = g_in.astype(f32)
    keep[2] = reach
    inner_map[...] = x_in


def weights_body(kerr, wave, kerr_b, wave_b):
    xs, ys, cols = kerr_b.shape
    kt, wt = kerr[...].T, wave[...].T
    for x in range(xs):
        kerr_b[x] = jnp.broadcast_to(kt[:, x : x + 1], (ys, cols))
        wave_b[x] = jnp.broadcast_to(wt[:, x : x + 1], (ys, cols))


def profiles(xs):
    i = lax.broadcasted_iota(jnp.int32, (xs, 1), 0).astype(f32)
    return (xs - i) / xs, (i + 1.0) / xs


def edge_columns(ends, w, z, pair, cross):
    xs = pair.shape[0]
    ys = w.shape[0]
    lp, rp = profiles(xs)
    low = ends[0:xs, :] + (lp * w[0:1, :] + rp * z[0:1, :])
    high = ends[xs:, :] + (lp * w[ys - 1 : ys, :] + rp * z[ys - 1 : ys, :])
    even = lax.axis_index("gy") % 2 == 0
    pair[...] = jnp.where(even, high, low).astype(bf16)
    cross[...] = jnp.where(even, low, high).astype(bf16)


def finish_body(count, got, keep, inner_map, ends, waves, halo, pair, cross):
    ys = got.shape[0] // 2
    xs = pair.shape[0]
    place = lax.axis_index("gx")
    inner = (place == count // 2 - 1) | (place == count // 2)
    is_a = place < count // 2
    back = got[0:ys, :]
    e_got = got[ys:, :].astype(f32)
    f_out, g_in, reach = keep[0], keep[1], keep[2]
    t = lax.dot_general(
        inner_map[...], back, (((0,), (0,)), ((), ())), preferred_element_type=f32
    ) + g_in
    back = back.astype(f32)
    forward = jnp.where(inner, f_out, 0.0)
    backward = jnp.where(inner, back, t)
    w = lift_weight * jnp.where(is_a, forward, backward)
    z = lift_weight * jnp.where(is_a, backward, forward)
    waves[0] = w
    waves[1] = z
    toward = jnp.where(
        inner,
        e_got + lift_weight * reach,
        g_in + lift_weight * (f_out + back * (1.0 / xs)),
    )
    away = jnp.where(inner, f_out + lift_weight * t, 0.0)
    halo[0] = jnp.where(is_a, away, toward).astype(bf16)
    halo[1] = jnp.where(is_a, toward, away).astype(bf16)
    edge_columns(ends, w, z, pair, cross)


def ends_body(ends, waves, pair, cross):
    edge_columns(ends, waves[0], waves[1], pair, cross)


def stencil(rows, ys):
    i = lax.broadcasted_iota(jnp.int32, (rows, rows), 0)
    j = lax.broadcasted_iota(jnp.int32, (rows, rows), 1)
    near = (abs(i - j) == 1) & (i // ys == j // ys)
    return jnp.where(i == j, -4.0, jnp.where(near, 1.0, 0.0)).astype(bf16)


def update_body(
    strip, group, part, waves, halo, kerr_b, wave_b, source, updated, residual, strips,
    u, res, sems,
):
    xs, ys, cols = source.shape
    w, z = waves[0], waves[1]
    u[0] = halo[0]
    u[xs + 1] = halo[1]

    def lift(x, _):
        xf = x.astype(f32)
        row = pl.multiple_of(x * ys, ys)
        lp, rp = (xs - xf) * (1.0 / xs), (xf + 1.0) * (1.0 / xs)
        u[x + 1] = (part[pl.ds(row, ys), :] + (lp * w + rp * z)).astype(bf16)
        return 0

    lax.fori_loop(0, xs, lift, 0, unroll=4)
    out_u = pltpu.make_async_copy(u.at[pl.ds(1, xs)], updated, sems.at[0])
    out_u.start()
    taps = stencil(group * ys, ys)

    def one(i, _):
        x = i * group
        mid = u[pl.ds(x + 1, group)]
        near = matmul(taps, mid.reshape(group * ys, cols)).reshape(group, ys, cols)
        m = mid.astype(f32)
        above = u[pl.ds(x, group)].astype(f32)
        below = u[pl.ds(x + 2, group)].astype(f32)
        k, v = kerr_b[pl.ds(x, group)], wave_b[pl.ds(x, group)]
        s = source[pl.ds(x, group)].astype(f32)
        r = (near + (above + below)) + (m * (v + k * (m * m)) - s)
        strips[0, pl.ds(x, group)] = r[:, :strip, :]
        strips[1, pl.ds(x, group)] = r[:, ys - strip :, :]
        res[pl.ds(x, group)] = r[:, strip : ys - strip, :].astype(bf16)
        return 0

    lax.fori_loop(0, xs // group, one, 0)
    out_r = pltpu.make_async_copy(res, residual.at[:, pl.ds(strip, ys - 2 * strip), :], sems.at[1])
    out_r.start()
    out_u.wait()
    out_r.wait()


def seam_body(count, strip, strips, pair, cross, _, residual, work, out, sems):
    xs, ys, cols = residual.shape
    g = lax.axis_index("gy")
    even = g % 2 == 0
    zero = jnp.zeros((), f32)
    p, c = pair[...].astype(f32), cross[...].astype(f32)
    low = jnp.where(g == 0, zero, jnp.where(even, c, p))
    high = jnp.where(g == count - 1, zero, jnp.where(even, p, c))
    for e, (row, add) in enumerate(((0, low), (strip - 1, high))):
        work[e] = strips[e].reshape(xs * strip, cols)
        at = pl.ds(row, xs, stride=strip)
        work[e, at, :] = work[e, at, :] + add
        out[e] = work[e].reshape(xs, strip, cols).astype(bf16)
        y0 = 0 if e == 0 else ys - strip
        pltpu.make_async_copy(
            out.at[e], residual.at[:, pl.ds(y0, strip), :], sems.at[e]
        ).start()
    for e in range(2):
        y0 = 0 if e == 0 else ys - strip
        pltpu.make_async_copy(
            out.at[e], residual.at[:, pl.ds(y0, strip), :], sems.at[e]
        ).wait()


def gathered_sweeps(message, ys, xs, count):
    place = lax.axis_index("gx")
    every = lax.all_gather(message, "gx").astype(f32)
    right, left = every[:, :ys], every[:, ys : 2 * ys]
    packed = every[:, 2 * ys :]
    maps = jnp.concatenate([packed[:, :, :ys], packed[:, :, ys:]], axis=1)
    start = jnp.zeros_like(right[0])
    exact = functools.partial(jnp.dot, precision=lax.Precision.HIGHEST)

    def up(state, inp):
        return exact(inp[0], state) + inp[1], state

    def down(state, inp):
        return exact(inp[0].T, state) + inp[1], state

    _, w = lax.scan(up, start, (maps, right))
    _, z = lax.scan(down, start, (maps, left), reverse=True)
    before, after = jnp.maximum(place - 1, 0), jnp.minimum(place + 1, count - 1)
    low = right[before] + lift_weight * (w[before] / xs + z[before])
    high = left[after] + lift_weight * (w[after] + z[after] / xs)
    low = jnp.where(place == 0, 0.0, low)
    high = jnp.where(place == count - 1, 0.0, high)
    return lift_weight * jnp.stack([w[place], z[place]]), jnp.stack([low, high]).astype(bf16)


def per_device(source, field, kerr, wave, leaf_ops, transfer_ops):
    xs, ys, cols = source.shape
    lx, ly, pts, _ = leaf_ops.shape
    points = xs // lx
    n_gx, n_gy = lax.axis_size("gx"), lax.axis_size("gy")
    doubling = n_gx == 4
    shape = jax.ShapeDtypeStruct
    dots = 2 * lx * ly * pts * pts * cols

    message, edge = call(
        functools.partial(faces_body, n_gx // 2 if doubling else n_gx, points),
        (shape((2 * ys + ys // 2, cols), bf16), shape((2, points, ys, cols), bf16)),
        [ANY, ANY, VMEM, ANY, VMEM],
        scratch=[
            pltpu.VMEM((2, points, ys, cols), bf16),
            pltpu.VMEM((2, points, ys, cols), bf16),
            pltpu.VMEM((2, ly, points, pts), bf16),
            pltpu.SemaphoreType.DMA((2, 3)),
        ],
        cost=(dots // 8, 2 << 20),
    )(source, field, kerr, leaf_ops, transfer_ops)

    if doubling:
        other = lax.ppermute(message, "gx", [(i, i ^ 1) for i in range(n_gx)])

    part, ends = call(
        functools.partial(leaves_body, points),
        (shape((xs * ys, cols), f32), shape((2 * xs, cols), f32)),
        [VMEM] * 5,
        scratch=[pltpu.VMEM((xs, ys, cols), bf16)],
        cost=(dots, 6 << 20),
    )(edge, source, field, kerr, leaf_ops)

    kerr_b, wave_b = call(
        weights_body,
        (shape((xs, ys, cols), f32), shape((xs, ys, cols), f32)),
        [VMEM] * 2,
        cost=(xs * ys * cols, 4 << 20),
    )(kerr, wave)

    column = shape((xs, cols), bf16)
    if doubling:
        reach, keep, inner_map = call(
            functools.partial(compose_body, n_gx, xs),
            (shape((2 * ys, cols), bf16), shape((3, ys, cols), f32), shape((ys, ys), bf16)),
            [VMEM] * 2,
        )(message, other)
        far = lax.ppermute(reach, "gx", [(i, i ^ 2) for i in range(n_gx)])
        waves, halo, pair, cross = call(
            functools.partial(finish_body, n_gx),
            (shape((2, ys, cols), f32), shape((2, ys, cols), bf16), column, column),
            [VMEM] * 4,
        )(far, keep, inner_map, ends)
    else:
        waves, halo = gathered_sweeps(message, ys, xs, n_gx)
        pair, cross = call(ends_body, (column, column), [VMEM] * 2)(ends, waves)

    pair_to = [(i, i + 1 - 2 * (i % 2)) for i in range(n_gy)]
    cross_to = [(i, (i - 1 + 2 * (i % 2)) % n_gy) for i in range(n_gy)]
    pair = lax.ppermute(pair, "gy", pair_to)
    cross = lax.ppermute(cross, "gy", cross_to)

    strip, group = 16, 4
    big = shape((xs, ys, cols), bf16)
    updated, residual, strips = call(
        functools.partial(update_body, strip, group),
        (big, big, shape((2, xs, strip, cols), f32)),
        [VMEM] * 6,
        out_specs=(ANY, ANY, VMEM),
        scratch=[
            pltpu.VMEM((xs + 2, ys, cols), bf16),
            pltpu.VMEM((xs, ys - 2 * strip, cols), bf16),
            pltpu.SemaphoreType.DMA((2,)),
        ],
        cost=(20 * xs * ys * cols, 10 << 20),
    )(part, waves, halo, kerr_b, wave_b, source)

    residual = call(
        functools.partial(seam_body, n_gy, strip),
        big,
        [VMEM, VMEM, VMEM, ANY],
        out_specs=ANY,
        scratch=[
            pltpu.VMEM((2, xs * strip, cols), f32),
            pltpu.VMEM((2, xs, strip, cols), bf16),
            pltpu.SemaphoreType.DMA((2,)),
        ],
        aliases={3: 0},
    )(strips, pair, cross, residual)
    return updated, residual


def solution(mesh):
    return jax.shard_map(
        per_device,
        mesh=mesh,
        in_specs=(
            P(("grp", "gx"), "gy", None),
            P(("grp", "gx"), "gy", None),
            P(("grp", "gx"), "gy"),
            P(("grp", "gx"), "gy"),
            P("gx", "gy", None, None),
            P("gx", "gy", None),
        ),
        out_specs=(P(("grp", "gx"), "gy", None), P(("grp", "gx"), "gy", None)),
        check_vma=False,
    )
```

time: 93 us -> 26.4 us (0.28)
  the two profiles are of different devices: /device:TPU:1 before, /device:TPU:0 now
where the time goes in v1:
time: 26.4 us; the launch traced here: 26.1 us
  Pallas kernels  8.97 us (34%)
  starting transfers between devices  8.14 us (31%)
  local copies, waits for them, and re-layouts  5.56 us (21%)
  waiting for transfers between devices  2.7 us (10%)
  between operations  0.71 us (3%)
    pallas_call x7, Pallas kernels, run(): pl.pallas_call(body, out_shape=outs, in_specs=ins, out_specs=out_specs if...  8.97 us
    unnamed x16, local copies, waits for them, and re-layouts  5.56 us
    ppermute x1, starting transfers between devices, per_device(): other = lax.ppermute(message, 'gx', [(i, i ^ 1) for i in range(n_gx)])  3.09 us
    ppermute x1, starting transfers between devices, per_device(): far = lax.ppermute(reach, 'gx', [(i, i ^ 2) for i in range(n_gx)])  3.05 us
    ppermute x1, waiting for transfers between devices, per_device(): other = lax.ppermute(message, 'gx', [(i, i ^ 1) for i in range(n_gx)])  1.98 us
    ppermute x1, starting transfers between devices, per_device(): cross = lax.ppermute(cross, 'gy', cross_to)  1.94 us
    ppermute x1, waiting for transfers between devices, per_device(): far = lax.ppermute(reach, 'gx', [(i, i ^ 2) for i in range(n_gx)])  0.71 us
  transfers between devices with their start and end apart: 4, of which 2 were waited for; matrix products, arithmetic and copies ran while one was open for 0% of the time, Pallas kernels for 25%

profile of v1, /device:TPU:0, one launch (start us, length us, event | category | flops | bytes accessed | tf_op | source)
XLA Modules:
  0.0 26.1 jit_solution(18217994901599597040)
XLA Ops:
  0.6 0.0 copy-start
  0.6 1.2 %copy-done = bf16[64,64,128]{2,1,0:T(8,128)(2,1)S(1)} copy-done((bf16[64,64,128]{2,1,0:T(8,128)(2,1)S(1)}, bf16[64,64,128]{2,1,0:T(8,128)(2,1)}, u32[]{:S(2)}) %copy-start) | copy-done | bytes 1048600
  1.9 0.0 copy-start.2
  1.9 1.6 %copy-done.2 = bf16[4,4,256,256]{3,2,1,0:T(8,128)(2,1)S(1)} copy-done((bf16[4,4,256,256]{3,2,1,0:T(8,128)(2,1)S(1)}, bf16[4,4,256,256]{3,2,1,0:T(8,128)(2,1)}, u32[]{:S(2)}) %copy-start.2) | copy-done | bytes 2097176
  3.4 0.0 copy-start.3
  3.5 1.2 %copy-done.3 = bf16[64,64,128]{2,1,0:T(8,128)(2,1)S(1)} copy-done((bf16[64,64,128]{2,1,0:T(8,128)(2,1)S(1)}, bf16[64,64,128]{2,1,0:T(8,128)(2,1)}, u32[]{:S(2)}) %copy-start.3) | copy-done | bytes 1048600
  4.7 0.0 copy-start.4
  4.7 0.8 %copy-done.4 = f32[64,64]{1,0:T(8,128)S(1)} copy-done((f32[64,64]{1,0:T(8,128)S(1)}, f32[64,64]{1,0:T(8,128)}, u32[]{:S(2)}) %copy-start.4) | copy-done | bytes 16408
  5.4 0.0 copy-start.6
  5.4 0.8 %copy-done.6 = f32[1,64,64]{2,1,0:T(8,128)S(1)} copy-done((f32[1,64,64]{2,1,0:T(8,128)S(1)}, f32[1,64,64]{2,1,0:T(8,128)}, u32[]{:S(2)}) %copy-start.6) | copy-done | bytes 16408
  6.2 0.0 copy-start.1
  6.2 1.0 %shard_map.77 = (bf16[160,128]{1,0:T(8,128)(2,1)S(1)}, bf16[2,16,64,128]{3,2,1,0:T(8,128)(2,1)S(1)}) custom-call(bf16[64,64,128]{2,1,0:T(8,128)(2,1)S(1)} %copy-done, bf16[64,64,128]{2,1,0:T(8,128)(2,1)S(1)} %copy-done.3, f32[64,64]{1,0:T(8,128)S(1)} %copy-done.4, bf16[4,4,256,256]{3,2,1,0:T(8,128)(2,1)S(1)} %copy-done.2, f32[1,64,64]{2,1,0:T(8,128)S(1)} %copy-done.6), custom_call_target="tpu_custom_call" | custom-call | flops 33554432 | bytes 2097152 | tf_op jit(solution)/shard_map/pallas_call | solution.py:18
  7.2 3.1 %collective-permute-start = (bf16[160,128]{1,0:T(8,128)(2,1)S(1)}, bf16[160,128]{1,0:T(8,128)(2,1)S(1)}, u32[]{:S(2)}, u32[]{:S(2)}) collective-permute-start(bf16[160,128]{1,0:T(8,128)(2,1)S(1)} %get-tuple-element.20.own), channel_id=1, source_target_pairs={{0,4},{4,0},{8,12},{12,8},{1,5},{5,1},{9,13},{13,9},{2,6},{6,2},{1... | collective-permute-start | bytes 122888 | tf_op jit(solution)/shard_map/ppermute | solution.py:310
  10.3 2.0 %collective-permute-done.got = bf16[160,128]{1,0:T(8,128)(2,1)S(1)} collective-permute-done((bf16[160,128]{1,0:T(8,128)(2,1)S(1)}, bf16[160,128]{1,0:T(8,128)(2,1)S(1)}, u32[]{:S(2)}, u32[]{:S(2)}) %collective-permute-start) | collective-permute-done | bytes 40992 | tf_op jit(solution)/shard_map/ppermute | solution.py:310
  12.3 0.2 shard_map.79
  12.5 3.0 %collective-permute-start.1 = (bf16[128,128]{1,0:T(8,128)(2,1)S(1)}, bf16[128,128]{1,0:T(8,128)(2,1)S(1)}, u32[]{:S(2)}, u32[]{:S(2)}) collective-permute-start(bf16[128,128]{1,0:T(8,128)(2,1)S(1)} %get-tuple-element.21), channel_id=1, source_target_pairs={{0,8},{4,12},{8,0},{12,4},{1,9},{5,13},{9,1},{13,5},{2,10},{6,14},... | collective-permute-start | bytes 98312 | tf_op jit(solution)/shard_map/ppermute | solution.py:334
  15.6 0.0 copy-done.1
  15.6 0.0 copy-start.5
  15.6 0.0 copy-start.7
  15.6 1.2 %shard_map.78 = (f32[4096,128]{1,0:T(8,128)S(1)}, f32[128,128]{1,0:T(8,128)S(1)}) custom-call(bf16[2,16,64,128]{3,2,1,0:T(8,128)(2,1)S(1)} %get-tuple-element.18.edge, bf16[64,64,128]{2,1,0:T(8,128)(2,1)S(1)} %copy-done.1, bf16[64,64,128]{2,1,0:T(8,128)(2,1)S(1)} %copy-done.3, f32[64,64]{1,0:T(8,128)S(1)} %copy-done.4, bf16[4,4,256,256]{3,2,1,0:T(8,128)(2,1)S(1)} %copy-done.2), custom_call_target="tpu_custom_call" | custom-call | flops 268435456 | bytes 6291456 | tf_op jit(solution)/shard_map/pallas_call | solution.py:18
  16.7 0.7 %collective-permute-done.1.got = bf16[128,128]{1,0:T(8,128)(2,1)S(1)} collective-permute-done((bf16[128,128]{1,0:T(8,128)(2,1)S(1)}, bf16[128,128]{1,0:T(8,128)(2,1)S(1)}, u32[]{:S(2)}, u32[]{:S(2)}) %collective-permute-start.1) | collective-permute-done | bytes 32800 | tf_op jit(solution)/shard_map/ppermute | solution.py:334
  17.5 0.2 shard_map.80
  17.7 0.1 collective-permute-start.2
  17.7 1.9 %collective-permute-start.3 = (bf16[64,128]{1,0:T(8,128)(2,1)S(1)}, bf16[64,128]{1,0:T(8,128)(2,1)S(1)}, u32[]{:S(2)}, u32[]{:S(2)}) collective-permute-start(bf16[64,128]{1,0:T(8,128)(2,1)S(1)} %get-tuple-element.32), channel_id=1, source_target_pairs={{0,3},{1,2},{2,1},{3,0},{4,7},{5,6},{6,5},{7,4},{8,11},{9,10},{10,... | collective-permute-start | bytes 49160 | tf_op jit(solution)/shard_map/ppermute | solution.py:347
  19.7 0.0 copy-done.5
  19.7 0.0 copy-done.7
  19.7 1.3 %shard_map.81 = (f32[64,64,128]{2,1,0:T(8,128)S(1)}, f32[64,64,128]{2,1,0:T(8,128)S(1)}) custom-call(f32[64,64]{1,0:T(8,128)S(1)} %copy-done.5, f32[64,64]{1,0:T(8,128)S(1)} %copy-done.7), custom_call_target="tpu_custom_call" | custom-call | flops 524288 | bytes 4194304 | tf_op jit(solution)/shard_map/pallas_call | solution.py:18
  21.0 4.2 %shard_map.82 = (bf16[64,64,128]{2,1,0:T(8,128)(2,1)}, bf16[64,64,128]{2,1,0:T(8,128)(2,1)}, f32[2,64,16,128]{3,2,1,0:T(8,128)S(1)}) custom-call(f32[4096,128]{1,0:T(8,128)S(1)} %get-tuple-element.19.part, f32[2,64,128]{2,1,0:T(8,128)S(1)} %get-tuple-element.25.waves, bf16[2,64,128]{2,1,0:T(8,128)(2,1)S(1)} %get-tuple-element.26.halo, ...), custom_call_target="tpu_custom_call" | custom-call | flops 10485760 | bytes 10485760 | tf_op jit(solution)/shard_map/pallas_call | solution.py:18
  25.2 0.0 collective-permute-done.2.pair
  25.2 0.0 collective-permute-done.3.cross
  25.2 0.9 %shard_map.83 = bf16[64,64,128]{2,1,0:T(8,128)(2,1)} custom-call(f32[2,64,16,128]{3,2,1,0:T(8,128)S(1)} %get-tuple-element.30.strips, bf16[64,128]{1,0:T(8,128)(2,1)S(1)} %collective-permute-done.2.pair, bf16[64,128]{1,0:T(8,128)(2,1)S(1)} %collective-permute-done.3.cross, bf16[64,64,128]{2,1,0:T(8,128)(2,1)} %get-tuple-element.33._), custom_call_target="tpu_custom_call", output_to_operand_aliasing={{}: (3, {})} | custom-call | tf_op jit(solution)/shard_map/pallas_call | solution.py:18
Async XLA Ops:
  0.6 1.2 %copy-start = (bf16[64,64,128]{2,1,0:T(8,128)(2,1)S(1)}, bf16[64,64,128]{2,1,0:T(8,128)(2,1)}, u32[]{:S(2)}) copy-start(bf16[64,64,128]{2,1,0:T(8,128)(2,1)} %source.5) | copy-start | bytes 3145732
  1.9 1.6 %copy-start.2 = (bf16[4,4,256,256]{3,2,1,0:T(8,128)(2,1)S(1)}, bf16[4,4,256,256]{3,2,1,0:T(8,128)(2,1)}, u32[]{:S(2)}) copy-start(bf16[4,4,256,256]{3,2,1,0:T(8,128)(2,1)} %leaf_ops.3) | copy-start | bytes 6291460
  3.4 1.2 %copy-start.3 = (bf16[64,64,128]{2,1,0:T(8,128)(2,1)S(1)}, bf16[64,64,128]{2,1,0:T(8,128)(2,1)}, u32[]{:S(2)}) copy-start(bf16[64,64,128]{2,1,0:T(8,128)(2,1)} %field.3) | copy-start | bytes 3145732
  4.7 0.8 %copy-start.4 = (f32[64,64]{1,0:T(8,128)S(1)}, f32[64,64]{1,0:T(8,128)}, u32[]{:S(2)}) copy-start(f32[64,64]{1,0:T(8,128)} %kerr.5) | copy-start | bytes 49156
  5.4 0.8 %copy-start.6 = (f32[1,64,64]{2,1,0:T(8,128)S(1)}, f32[1,64,64]{2,1,0:T(8,128)}, u32[]{:S(2)}) copy-start(f32[1,64,64]{2,1,0:T(8,128)} %transfer.1) | copy-start | bytes 49156
  6.2 9.4 %copy-start.1 = (bf16[64,64,128]{2,1,0:T(8,128)(2,1)S(1)}, bf16[64,64,128]{2,1,0:T(8,128)(2,1)}, u32[]{:S(2)}) copy-start(bf16[64,64,128]{2,1,0:T(8,128)(2,1)} %source.5) | copy-start | bytes 3145732
  7.2 5.1 %collective-permute-start = (bf16[160,128]{1,0:T(8,128)(2,1)S(1)}, bf16[160,128]{1,0:T(8,128)(2,1)S(1)}, u32[]{:S(2)}, u32[]{:S(2)}) collective-permute-start(bf16[160,128]{1,0:T(8,128)(2,1)S(1)} %get-tuple-element.20.own), channel_id=1, source_target_pairs={{0,4},{4,0},{8,12},{12,8},{1,5},{5,1},{9,13},{13,9},{2,6},{6,2},{1... | collective-permute-start | bytes 122888 | tf_op jit(solution)/shard_map/ppermute | solution.py:310
  12.5 4.9 %collective-permute-start.1 = (bf16[128,128]{1,0:T(8,128)(2,1)S(1)}, bf16[128,128]{1,0:T(8,128)(2,1)S(1)}, u32[]{:S(2)}, u32[]{:S(2)}) collective-permute-start(bf16[128,128]{1,0:T(8,128)(2,1)S(1)} %get-tuple-element.21), channel_id=1, source_target_pairs={{0,8},{4,12},{8,0},{12,4},{1,9},{5,13},{9,1},{13,5},{2,10},{6,14},... | collective-permute-start | bytes 98312 | tf_op jit(solution)/shard_map/ppermute | solution.py:334
  15.6 4.1 %copy-start.5 = (f32[64,64]{1,0:T(8,128)S(1)}, f32[64,64]{1,0:T(8,128)}, u32[]{:S(2)}) copy-start(f32[64,64]{1,0:T(8,128)} %kerr.5) | copy-start | bytes 49156
  15.6 4.1 %copy-start.7 = (f32[64,64]{1,0:T(8,128)S(1)}, f32[64,64]{1,0:T(8,128)}, u32[]{:S(2)}) copy-start(f32[64,64]{1,0:T(8,128)} %wave.1) | copy-start | bytes 49156
  17.7 7.5 %collective-permute-start.2 = (bf16[64,128]{1,0:T(8,128)(2,1)S(1)}, bf16[64,128]{1,0:T(8,128)(2,1)S(1)}, u32[]{:S(2)}, u32[]{:S(2)}) collective-permute-start(bf16[64,128]{1,0:T(8,128)(2,1)S(1)} %get-tuple-element.31), channel_id=1, source_target_pairs={{0,1},{1,0},{2,3},{3,2},{4,5},{5,4},{6,7},{7,6},{8,9},{9,8},{10,11... | collective-permute-start | bytes 49160 | tf_op jit(solution)/shard_map/ppermute | solution.py:346
  17.7 7.4 %collective-permute-start.3 = (bf16[64,128]{1,0:T(8,128)(2,1)S(1)}, bf16[64,128]{1,0:T(8,128)(2,1)S(1)}, u32[]{:S(2)}, u32[]{:S(2)}) collective-permute-start(bf16[64,128]{1,0:T(8,128)(2,1)S(1)} %get-tuple-element.32), channel_id=1, source_target_pairs={{0,3},{1,2},{2,1},{3,0},{4,7},{5,6},{6,5},{7,4},{8,11},{9,10},{10,... | collective-permute-start | bytes 49160 | tf_op jit(solution)/shard_map/ppermute | solution.py:347

commit v2 on v1

--- a/solution.py
+++ b/solution.py
@@ -11,6 +11,7 @@
 f32, bf16 = jnp.float32, jnp.bfloat16
 VMEM = pl.BlockSpec(memory_space=pltpu.VMEM)
 ANY = pl.BlockSpec(memory_space=pl.ANY)
+HBM = pl.BlockSpec(memory_space=pltpu.HBM)
 
 
 def call(body, outs, ins, out_specs=None, scratch=(), cost=(0, 0), aliases=None):
@@ -31,6 +32,10 @@
     return run
 
 
+def in_hbm(x):
+    return pltpu.with_memory_space_constraint(x, pltpu.HBM)
+
+
 def matmul(a, b):
     return jnp.dot(a, b, preferred_element_type=f32)
 
@@ -41,10 +46,16 @@
 
 
 def faces_body(
-    half, points, source, field, kerr, leaf_ops, transfer, msg, edge, src, fld, ops, sems
+    half, points, source, field, kerr_all, leaf_ops, transfer, msg, edge, src, fld, ops, kerr, own,
+    sems, more,
 ):
     lx, ly, pts, _ = leaf_ops.shape
     xs, ys, cols = source.shape
+    small = [
+        pltpu.make_async_copy(kerr_all, kerr, more.at[0]),
+        pltpu.make_async_copy(transfer.at[0], own, more.at[1]),
+    ]
+    small[0].start()
     copies = []
     for e, (x0, a, r0) in enumerate(((0, 0, 0), (xs - points, lx - 1, pts - points))):
         group = [
@@ -57,9 +68,9 @@
         for c in group:
             c.start()
         copies.append(group)
+    small[1].start()
     is_a = lax.axis_index("gx") < half
-    own = transfer[0]
-    x_map = jnp.where(is_a, own, own.T).astype(bf16)
+    small[0].wait()
     faces = []
     for e in range(2):
         x0 = 0 if e == 0 else xs - points
@@ -74,6 +85,8 @@
             rows.append(matmul(ops[e, b], rhs))
         faces.append(jnp.concatenate(rows, axis=0).astype(bf16))
     left, right = faces
+    small[1].wait()
+    x_map = jnp.where(is_a, own[...], own[...].T).astype(bf16)
     msg[0:ys, :] = jnp.where(is_a, right, left)
     msg[ys : 2 * ys, :] = jnp.where(is_a, left, right)
     msg[2 * ys :, :] = jnp.concatenate([x_map[: ys // 2], x_map[ys // 2 :]], axis=1)
@@ -296,15 +309,21 @@
     message, edge = call(
         functools.partial(faces_body, n_gx // 2 if doubling else n_gx, points),
         (shape((2 * ys + ys // 2, cols), bf16), shape((2, points, ys, cols), bf16)),
-        [ANY, ANY, VMEM, ANY, VMEM],
+        [HBM] * 5,
         scratch=[
             pltpu.VMEM((2, points, ys, cols), bf16),
             pltpu.VMEM((2, points, ys, cols), bf16),
             pltpu.VMEM((2, ly, points, pts), bf16),
+            pltpu.VMEM((xs, ys), f32),
+            pltpu.VMEM((ys, ys), f32),
             pltpu.SemaphoreType.DMA((2, 3)),
+            pltpu.SemaphoreType.DMA((2,)),
         ],
         cost=(dots // 8, 2 << 20),
-    )(source, field, kerr, leaf_ops, transfer_ops)
+    )(*map(in_hbm, (source, field, kerr, leaf_ops, transfer_ops)))
+    message, edge, source, field, kerr, wave, leaf_ops = lax.optimization_barrier(
+        (message, edge, source, field, kerr, wave, leaf_ops)
+    )
 
     if doubling:
         other = lax.ppermute(message, "gx", [(i, i ^ 1) for i in range(n_gx)])
@@ -326,12 +345,14 @@
 
     column = shape((xs, cols), bf16)
     if doubling:
+        other, part, ends = lax.optimization_barrier((other, part, ends))
         reach, keep, inner_map = call(
             functools.partial(compose_body, n_gx, xs),
             (shape((2 * ys, cols), bf16), shape((3, ys, cols), f32), shape((ys, ys), bf16)),
             [VMEM] * 2,
         )(message, other)
         far = lax.ppermute(reach, "gx", [(i, i ^ 2) for i in range(n_gx)])
+        far, kerr_b, wave_b = lax.optimization_barrier((far, kerr_b, wave_b))
         waves, halo, pair, cross = call(
             functools.partial(finish_body, n_gx),
             (shape((2, ys, cols), f32), shape((2, ys, cols), bf16), column, column),

time: 26.4 us -> 20.6 us (0.78)
  local copies, waits for them, and re-layouts: 5.56 us -> 0.02 us
  waiting for transfers between devices: 2.7 us -> 1.37 us
  Pallas kernels: 8.97 us -> 10.2 us
    unnamed x16 -> x10, local copies, waits for them, and re-layouts: 5.56 us -> 0.02 us
    pallas_call x7, Pallas kernels: 8.97 us -> 10.2 us  [run(): pl.pallas_call(body, out_shape=outs, in_specs=ins, out_specs=out_specs if...]
    ppermute x1, waiting for transfers between devices: 1.98 us -> 0.79 us  [per_device(): other = lax.ppermute(message, 'gx', [(i, i ^ 1) for i in range(n_gx)])]
  transfers between devices with their start and end apart: 4 -> 4, of which waited for: 2 -> 2; matrix products, arithmetic and copies ran while one was open for 0% -> 0% of each run, Pallas kernels for 25% -> 32%
where the time goes in v2:
time: 20.6 us; the launch traced here: 20.5 us
  Pallas kernels  10.2 us (50%)
  starting transfers between devices  8.14 us (40%)
  waiting for transfers between devices  1.37 us (7%)
  between operations  0.74 us (4%)
    pallas_call x7, Pallas kernels, run(): pl.pallas_call(body, out_shape=outs, in_specs=ins, out_specs=out_specs if...  10.2 us
    ppermute x1, starting transfers between devices, per_device(): other = lax.ppermute(message, 'gx', [(i, i ^ 1) for i in range(n_gx)])  3.09 us
    ppermute x1, starting transfers between devices, per_device(): far = lax.ppermute(reach, 'gx', [(i, i ^ 2) for i in range(n_gx)])  3.05 us
    ppermute x1, starting transfers between devices, per_device(): cross = lax.ppermute(cross, 'gy', cross_to)  1.94 us
    ppermute x1, waiting for transfers between devices, per_device(): other = lax.ppermute(message, 'gx', [(i, i ^ 1) for i in range(n_gx)])  0.79 us
    ppermute x1, waiting for transfers between devices, per_device(): far = lax.ppermute(reach, 'gx', [(i, i ^ 2) for i in range(n_gx)])  0.58 us
  transfers between devices with their start and end apart: 4, of which 2 were waited for; matrix products, arithmetic and copies ran while one was open for 0% of the time, Pallas kernels for 32%

profile of v2, /device:TPU:0, one launch (start us, length us, event | category | flops | bytes accessed | tf_op | source)
XLA Modules:
  0.0 20.5 jit_solution(7123176884092390797)
XLA Ops:
  0.6 0.0 copy-start.1
  0.6 0.0 copy-start.3
  0.7 0.0 copy-start.2
  0.7 0.0 copy-start
  0.7 2.3 %shard_map.77 = (bf16[160,128]{1,0:T(8,128)(2,1)S(1)}, bf16[2,16,64,128]{3,2,1,0:T(8,128)(2,1)S(1)}) custom-call(bf16[64,64,128]{2,1,0:T(8,128)(2,1)} %source.3, bf16[64,64,128]{2,1,0:T(8,128)(2,1)} %field.2, f32[64,64]{1,0:T(8,128)} %kerr.1, bf16[4,4,256,256]{3,2,1,0:T(8,128)(2,1)} %leaf_ops.2, f32[1,64,64]{2,1,0:T(8,128)} %transfer.1), custom_call_target="tpu_custom_call" | custom-call | flops 33554432 | bytes 2097152 | tf_op jit(solution)/shard_map/pallas_call | solution.py:19
  3.0 0.0 copy-start.4
  3.0 3.1 %collective-permute-start = (bf16[160,128]{1,0:T(8,128)(2,1)S(1)}, bf16[160,128]{1,0:T(8,128)(2,1)S(1)}, u32[]{:S(2)}, u32[]{:S(2)}) collective-permute-start(bf16[160,128]{1,0:T(8,128)(2,1)S(1)} %get-tuple-element.33.own), channel_id=1, source_target_pairs={{0,4},{4,0},{8,12},{12,8},{1,5},{5,1},{9,13},{13,9},{2,6},{6,2},{1... | collective-permute-start | bytes 122888 | tf_op jit(solution)/shard_map/ppermute | solution.py:329
  6.1 0.0 copy-done.1
  6.1 0.0 copy-done.3
  6.1 0.0 copy-done.2
  6.1 0.0 copy-done
  6.1 1.2 %shard_map.78 = (f32[4096,128]{1,0:T(8,128)S(1)}, f32[128,128]{1,0:T(8,128)S(1)}) custom-call(bf16[2,16,64,128]{3,2,1,0:T(8,128)(2,1)S(1)} %get-tuple-element.34.edge, bf16[64,64,128]{2,1,0:T(8,128)(2,1)S(1)} %copy-done, bf16[64,64,128]{2,1,0:T(8,128)(2,1)S(1)} %copy-done.2, f32[64,64]{1,0:T(8,128)S(1)} %copy-done.3, bf16[4,4,256,256]{3,2,1,0:T(8,128)(2,1)S(1)} %copy-done.1), custom_call_target="tpu_custom_call" | custom-call | flops 268435456 | bytes 6291456 | tf_op jit(solution)/shard_map/pallas_call | solution.py:19
  7.3 0.8 %collective-permute-done.got = bf16[160,128]{1,0:T(8,128)(2,1)S(1)} collective-permute-done((bf16[160,128]{1,0:T(8,128)(2,1)S(1)}, bf16[160,128]{1,0:T(8,128)(2,1)S(1)}, u32[]{:S(2)}, u32[]{:S(2)}) %collective-permute-start) | collective-permute-done | bytes 40992 | tf_op jit(solution)/shard_map/ppermute | solution.py:329
  8.1 0.2 shard_map.79
  8.2 3.0 %collective-permute-start.1 = (bf16[128,128]{1,0:T(8,128)(2,1)S(1)}, bf16[128,128]{1,0:T(8,128)(2,1)S(1)}, u32[]{:S(2)}, u32[]{:S(2)}) collective-permute-start(bf16[128,128]{1,0:T(8,128)(2,1)S(1)} %get-tuple-element.43), channel_id=1, source_target_pairs={{0,8},{4,12},{8,0},{12,4},{1,9},{5,13},{9,1},{13,5},{2,10},{6,14},... | collective-permute-start | bytes 98312 | tf_op jit(solution)/shard_map/ppermute | solution.py:354
  11.3 0.0 copy-done.4
  11.3 1.3 %shard_map.80 = (f32[64,64,128]{2,1,0:T(8,128)S(1)}, f32[64,64,128]{2,1,0:T(8,128)S(1)}) custom-call(f32[64,64]{1,0:T(8,128)S(1)} %copy-done.3, f32[64,64]{1,0:T(8,128)S(1)} %copy-done.4), custom_call_target="tpu_custom_call" | custom-call | flops 524288 | bytes 4194304 | tf_op jit(solution)/shard_map/pallas_call | solution.py:19
  12.6 0.6 %collective-permute-done.1.got = bf16[128,128]{1,0:T(8,128)(2,1)S(1)} collective-permute-done((bf16[128,128]{1,0:T(8,128)(2,1)S(1)}, bf16[128,128]{1,0:T(8,128)(2,1)S(1)}, u32[]{:S(2)}, u32[]{:S(2)}) %collective-permute-start.1) | collective-permute-done | bytes 32800 | tf_op jit(solution)/shard_map/ppermute | solution.py:354
  13.2 0.2 shard_map.81
  13.4 0.1 collective-permute-start.2
  13.5 1.9 %collective-permute-start.3 = (bf16[64,128]{1,0:T(8,128)(2,1)S(1)}, bf16[64,128]{1,0:T(8,128)(2,1)S(1)}, u32[]{:S(2)}, u32[]{:S(2)}) collective-permute-start(bf16[64,128]{1,0:T(8,128)(2,1)S(1)} %get-tuple-element.58), channel_id=1, source_target_pairs={{0,3},{1,2},{2,1},{3,0},{4,7},{5,6},{6,5},{7,4},{8,11},{9,10},{10,... | collective-permute-start | bytes 49160 | tf_op jit(solution)/shard_map/ppermute | solution.py:368
  15.4 4.2 %shard_map.82 = (bf16[64,64,128]{2,1,0:T(8,128)(2,1)}, bf16[64,64,128]{2,1,0:T(8,128)(2,1)}, f32[2,64,16,128]{3,2,1,0:T(8,128)S(1)}) custom-call(f32[4096,128]{1,0:T(8,128)S(1)} %get-tuple-element.41.part, f32[2,64,128]{2,1,0:T(8,128)S(1)} %get-tuple-element.51.waves, bf16[2,64,128]{2,1,0:T(8,128)(2,1)S(1)} %get-tuple-element.52.halo, ...), custom_call_target="tpu_custom_call" | custom-call | flops 10485760 | bytes 10485760 | tf_op jit(solution)/shard_map/pallas_call | solution.py:19
  19.6 0.0 collective-permute-done.2.pair
  19.6 0.0 collective-permute-done.3.cross
  19.6 0.9 %shard_map.83 = bf16[64,64,128]{2,1,0:T(8,128)(2,1)} custom-call(f32[2,64,16,128]{3,2,1,0:T(8,128)S(1)} %get-tuple-element.56.strips, bf16[64,128]{1,0:T(8,128)(2,1)S(1)} %collective-permute-done.2.pair, bf16[64,128]{1,0:T(8,128)(2,1)S(1)} %collective-permute-done.3.cross, bf16[64,64,128]{2,1,0:T(8,128)(2,1)} %get-tuple-element.59._), custom_call_target="tpu_custom_call", output_to_operand_aliasing={{}: (3, {})} | custom-call | tf_op jit(solution)/shard_map/pallas_call | solution.py:19
Async XLA Ops:
  0.6 5.4 %copy-start.1 = (bf16[4,4,256,256]{3,2,1,0:T(8,128)(2,1)S(1)}, bf16[4,4,256,256]{3,2,1,0:T(8,128)(2,1)}, u32[]{:S(2)}) copy-start(bf16[4,4,256,256]{3,2,1,0:T(8,128)(2,1)} %leaf_ops.2) | copy-start | bytes 6291460
  0.6 5.4 %copy-start.3 = (f32[64,64]{1,0:T(8,128)S(1)}, f32[64,64]{1,0:T(8,128)}, u32[]{:S(2)}) copy-start(f32[64,64]{1,0:T(8,128)} %kerr.1) | copy-start | bytes 49156
  0.7 5.4 %copy-start.2 = (bf16[64,64,128]{2,1,0:T(8,128)(2,1)S(1)}, bf16[64,64,128]{2,1,0:T(8,128)(2,1)}, u32[]{:S(2)}) copy-start(bf16[64,64,128]{2,1,0:T(8,128)(2,1)} %field.2) | copy-start | bytes 3145732
  0.7 5.4 %copy-start = (bf16[64,64,128]{2,1,0:T(8,128)(2,1)S(1)}, bf16[64,64,128]{2,1,0:T(8,128)(2,1)}, u32[]{:S(2)}) copy-start(bf16[64,64,128]{2,1,0:T(8,128)(2,1)} %source.3) | copy-start | bytes 3145732
  3.0 8.3 %copy-start.4 = (f32[64,64]{1,0:T(8,128)S(1)}, f32[64,64]{1,0:T(8,128)}, u32[]{:S(2)}) copy-start(f32[64,64]{1,0:T(8,128)} %wave) | copy-start | bytes 49156
  3.0 5.1 %collective-permute-start = (bf16[160,128]{1,0:T(8,128)(2,1)S(1)}, bf16[160,128]{1,0:T(8,128)(2,1)S(1)}, u32[]{:S(2)}, u32[]{:S(2)}) collective-permute-start(bf16[160,128]{1,0:T(8,128)(2,1)S(1)} %get-tuple-element.33.own), channel_id=1, source_target_pairs={{0,4},{4,0},{8,12},{12,8},{1,5},{5,1},{9,13},{13,9},{2,6},{6,2},{1... | collective-permute-start | bytes 122888 | tf_op jit(solution)/shard_map/ppermute | solution.py:329
  8.2 4.9 %collective-permute-start.1 = (bf16[128,128]{1,0:T(8,128)(2,1)S(1)}, bf16[128,128]{1,0:T(8,128)(2,1)S(1)}, u32[]{:S(2)}, u32[]{:S(2)}) collective-permute-start(bf16[128,128]{1,0:T(8,128)(2,1)S(1)} %get-tuple-element.43), channel_id=1, source_target_pairs={{0,8},{4,12},{8,0},{12,4},{1,9},{5,13},{9,1},{13,5},{2,10},{6,14},... | collective-permute-start | bytes 98312 | tf_op jit(solution)/shard_map/ppermute | solution.py:354
  13.4 6.2 %collective-permute-start.2 = (bf16[64,128]{1,0:T(8,128)(2,1)S(1)}, bf16[64,128]{1,0:T(8,128)(2,1)S(1)}, u32[]{:S(2)}, u32[]{:S(2)}) collective-permute-start(bf16[64,128]{1,0:T(8,128)(2,1)S(1)} %get-tuple-element.57), channel_id=1, source_target_pairs={{0,1},{1,0},{2,3},{3,2},{4,5},{5,4},{6,7},{7,6},{8,9},{9,8},{10,11... | collective-permute-start | bytes 49160 | tf_op jit(solution)/shard_map/ppermute | solution.py:367
  13.5 6.1 %collective-permute-start.3 = (bf16[64,128]{1,0:T(8,128)(2,1)S(1)}, bf16[64,128]{1,0:T(8,128)(2,1)S(1)}, u32[]{:S(2)}, u32[]{:S(2)}) collective-permute-start(bf16[64,128]{1,0:T(8,128)(2,1)S(1)} %get-tuple-element.58), channel_id=1, source_target_pairs={{0,3},{1,2},{2,1},{3,0},{4,7},{5,6},{6,5},{7,4},{8,11},{9,10},{10,... | collective-permute-start | bytes 49160 | tf_op jit(solution)/shard_map/ppermute | solution.py:368

commit v3 on v2

--- a/solution.py
+++ b/solution.py
@@ -46,49 +46,56 @@
 
 
 def faces_body(
-    half, points, source, field, kerr_all, leaf_ops, transfer, msg, edge, src, fld, ops, kerr, own,
-    sems, more,
+    half, points, parts, source, field, kerr_all, leaf_ops, transfer, msg, edge, src, fld, ops,
+    kerr, own, kb, sems, more,
 ):
     lx, ly, pts, _ = leaf_ops.shape
     xs, ys, cols = source.shape
-    small = [
-        pltpu.make_async_copy(kerr_all, kerr, more.at[0]),
-        pltpu.make_async_copy(transfer.at[0], own, more.at[1]),
-    ]
-    small[0].start()
-    copies = []
-    for e, (x0, a, r0) in enumerate(((0, 0, 0), (xs - points, lx - 1, pts - points))):
-        group = [
-            pltpu.make_async_copy(source.at[pl.ds(x0, points)], src.at[e], sems.at[e, 0]),
-            pltpu.make_async_copy(field.at[pl.ds(x0, points)], fld.at[e], sems.at[e, 1]),
-            pltpu.make_async_copy(
-                leaf_ops.at[a, :, pl.ds(r0, points), :], ops.at[e], sems.at[e, 2]
-            ),
-        ]
-        for c in group:
-            c.start()
-        copies.append(group)
-    small[1].start()
+    copy = pltpu.make_async_copy
+    firsts = (0, xs - points)
+    size = points // parts
+    coef = copy(kerr_all, kerr, more.at[0])
+    coef.start()
+    pieces = {}
+    for e, x0 in enumerate(firsts):
+        for i in range(parts):
+            at, here = pl.ds(x0 + i * size, size), pl.ds(i * size, size)
+            pieces[e, i] = (
+                copy(source.at[at], src.at[e, here], sems.at[e, 2 * i]),
+                copy(field.at[at], fld.at[e, here], sems.at[e, 2 * i + 1]),
+            )
+            for c in pieces[e, i]:
+                c.start(priority=e)
+    rows_of = []
+    for e, (a, r0) in enumerate(((0, 0), (lx - 1, pts - points))):
+        rows_of.append(copy(leaf_ops.at[a, :, pl.ds(r0, points), :], ops.at[e], more.at[2 + e]))
+        rows_of[e].start()
+    matrix = copy(transfer.at[0], own, more.at[1])
+    matrix.start()
     is_a = lax.axis_index("gx") < half
-    small[0].wait()
+    coef.wait()
+    kts = [kerr[x0 : x0 + points, :].T for x0 in firsts]
+    for e in range(2):
+        for q in range(points):
+            kb[e, q] = jnp.broadcast_to(kts[e][:, q : q + 1], (ys, cols))
     faces = []
     for e in range(2):
-        x0 = 0 if e == 0 else xs - points
-        kt = kerr[x0 : x0 + points, :].T
-        for c in copies[e]:
-            c.wait()
-        for q in range(points):
-            edge[e, q] = kerr_column(src[e, q], fld[e, q], kt[:, q : q + 1])
+        for i in range(parts):
+            for c in pieces[e, i]:
+                c.wait()
+            for q in range(i * size, (i + 1) * size):
+                edge[e, q] = kerr_column(src[e, q], fld[e, q], kb[e, q])
+        rows_of[e].wait()
         rows = []
         for b in range(ly):
             rhs = edge[e, :, b * points : (b + 1) * points, :].reshape(pts, cols)
             rows.append(matmul(ops[e, b], rhs))
         faces.append(jnp.concatenate(rows, axis=0).astype(bf16))
     left, right = faces
-    small[1].wait()
-    x_map = jnp.where(is_a, own[...], own[...].T).astype(bf16)
     msg[0:ys, :] = jnp.where(is_a, right, left)
     msg[ys : 2 * ys, :] = jnp.where(is_a, left, right)
+    matrix.wait()
+    x_map = jnp.where(is_a, own[...], own[...].T).astype(bf16)
     msg[2 * ys :, :] = jnp.concatenate([x_map[: ys // 2], x_map[ys // 2 :]], axis=1)
 
 
@@ -198,58 +205,75 @@
     edge_columns(ends, waves[0], waves[1], pair, cross)
 
 
-def stencil(rows, ys):
-    i = lax.broadcasted_iota(jnp.int32, (rows, rows), 0)
-    j = lax.broadcasted_iota(jnp.int32, (rows, rows), 1)
-    near = (abs(i - j) == 1) & (i // ys == j // ys)
-    return jnp.where(i == j, -4.0, jnp.where(near, 1.0, 0.0)).astype(bf16)
+def stencil(group, ys):
+    shape = (group * ys, (group + 2) * ys)
+    i = lax.broadcasted_iota(jnp.int32, shape, 0)
+    j = lax.broadcasted_iota(jnp.int32, shape, 1)
+    away = abs(i // ys + 1 - j // ys) + abs(i % ys - j % ys)
+    return jnp.where(away == 0, -4.0, jnp.where(away == 1, 1.0, 0.0)).astype(bf16)
 
 
 def update_body(
-    strip, group, part, waves, halo, kerr_b, wave_b, source, updated, residual, strips,
-    u, res, sems,
+    strip, group, chunk, last, part, waves, halo, kerr_b, wave_b, source, updated, residual,
+    strips, late, u, res, sems,
 ):
     xs, ys, cols = source.shape
     w, z = waves[0], waves[1]
     u[0] = halo[0]
     u[xs + 1] = halo[1]
-
-    def lift(x, _):
-        xf = x.astype(f32)
-        row = pl.multiple_of(x * ys, ys)
-        lp, rp = (xs - xf) * (1.0 / xs), (xf + 1.0) * (1.0 / xs)
-        u[x + 1] = (part[pl.ds(row, ys), :] + (lp * w + rp * z)).astype(bf16)
-        return 0
-
-    lax.fori_loop(0, xs, lift, 0, unroll=4)
-    out_u = pltpu.make_async_copy(u.at[pl.ds(1, xs)], updated, sems.at[0])
-    out_u.start()
-    taps = stencil(group * ys, ys)
-
-    def one(i, _):
-        x = i * group
-        mid = u[pl.ds(x + 1, group)]
-        near = matmul(taps, mid.reshape(group * ys, cols)).reshape(group, ys, cols)
-        m = mid.astype(f32)
-        above = u[pl.ds(x, group)].astype(f32)
-        below = u[pl.ds(x + 2, group)].astype(f32)
-        k, v = kerr_b[pl.ds(x, group)], wave_b[pl.ds(x, group)]
-        s = source[pl.ds(x, group)].astype(f32)
-        r = (near + (above + below)) + (m * (v + k * (m * m)) - s)
-        strips[0, pl.ds(x, group)] = r[:, :strip, :]
-        strips[1, pl.ds(x, group)] = r[:, ys - strip :, :]
-        res[pl.ds(x, group)] = r[:, strip : ys - strip, :].astype(bf16)
-        return 0
-
-    lax.fori_loop(0, xs // group, one, 0)
-    out_r = pltpu.make_async_copy(res, residual.at[:, pl.ds(strip, ys - 2 * strip), :], sems.at[1])
-    out_r.start()
-    out_u.wait()
-    out_r.wait()
-
-
-def seam_body(count, strip, strips, pair, cross, _, residual, work, out, sems):
+    taps = stencil(group, ys)
+    inside = pl.ds(strip, ys - 2 * strip)
+    copies = []
+
+    def send(src, dst):
+        copies.append(pltpu.make_async_copy(src, dst, sems.at[len(copies)]))
+        copies[-1].start()
+
+    def lift(x):
+        lp, rp = (xs - x) / xs, (x + 1) / xs
+        u[x + 1] = (part[x * ys : (x + 1) * ys, :] + (lp * w + rp * z)).astype(bf16)
+        if (x + 1) % chunk == 0:
+            at = pl.ds(x + 1 - chunk, chunk)
+            send(u.at[pl.ds(x + 2 - chunk, chunk)], updated.at[at])
+
+    def residue(x):
+        near = matmul(taps, u[x : x + group + 2].reshape((group + 2) * ys, cols))
+        for q in range(group):
+            m = u[x + q + 1].astype(f32)
+            s = source[x + q].astype(f32)
+            r = near[q * ys : (q + 1) * ys] + (m * (wave_b[x + q] + kerr_b[x + q] * (m * m)) - s)
+            strips[0, x + q] = r[:strip, :]
+            strips[1, x + q] = r[ys - strip :, :]
+            mid = r[strip : ys - strip, :].astype(bf16)
+            if x >= xs - last:
+                late[x + q - (xs - last)] = mid
+            else:
+                res[x + q] = mid
+        end = x + group
+        if end % chunk == 0 and end <= xs - last:
+            at = pl.ds(end - chunk, chunk)
+            send(res.at[at], residual.at[at, inside])
+
+    ahead = 64
+    for x in range(xs + ahead):
+        if x < xs:
+            lift(x)
+        if x >= ahead and (x - ahead) % group == 0:
+            residue(x - ahead)
+    for c in copies:
+        c.wait()
+
+
+def seam_body(count, strip, last, strips, late, pair, cross, _, residual, work, out, sems):
     xs, ys, cols = residual.shape
+    copies = [
+        pltpu.make_async_copy(
+            late,
+            residual.at[pl.ds(xs - last, last), pl.ds(strip, ys - 2 * strip)],
+            sems.at[2],
+        )
+    ]
+    copies[0].start()
     g = lax.axis_index("gy")
     even = g % 2 == 0
     zero = jnp.zeros((), f32)
@@ -262,14 +286,12 @@
         work[e, at, :] = work[e, at, :] + add
         out[e] = work[e].reshape(xs, strip, cols).astype(bf16)
         y0 = 0 if e == 0 else ys - strip
-        pltpu.make_async_copy(
-            out.at[e], residual.at[:, pl.ds(y0, strip), :], sems.at[e]
-        ).start()
-    for e in range(2):
-        y0 = 0 if e == 0 else ys - strip
-        pltpu.make_async_copy(
-            out.at[e], residual.at[:, pl.ds(y0, strip), :], sems.at[e]
-        ).wait()
+        copies.append(
+            pltpu.make_async_copy(out.at[e], residual.at[:, pl.ds(y0, strip), :], sems.at[e])
+        )
+        copies[-1].start()
+    for c in copies:
+        c.wait()
 
 
 def gathered_sweeps(message, ys, xs, count):
@@ -307,7 +329,7 @@
     dots = 2 * lx * ly * pts * pts * cols
 
     message, edge = call(
-        functools.partial(faces_body, n_gx // 2 if doubling else n_gx, points),
+        functools.partial(faces_body, n_gx // 2 if doubling else n_gx, points, 1),
         (shape((2 * ys + ys // 2, cols), bf16), shape((2, points, ys, cols), bf16)),
         [HBM] * 5,
         scratch=[
@@ -316,8 +338,9 @@
             pltpu.VMEM((2, ly, points, pts), bf16),
             pltpu.VMEM((xs, ys), f32),
             pltpu.VMEM((ys, ys), f32),
-            pltpu.SemaphoreType.DMA((2, 3)),
-            pltpu.SemaphoreType.DMA((2,)),
+            pltpu.VMEM((2, points, ys, cols), f32),
+            pltpu.SemaphoreType.DMA((2, 8)),
+            pltpu.SemaphoreType.DMA((4,)),
         ],
         cost=(dots // 8, 2 << 20),
     )(*map(in_hbm, (source, field, kerr, leaf_ops, transfer_ops)))
@@ -367,33 +390,38 @@
     pair = lax.ppermute(pair, "gy", pair_to)
     cross = lax.ppermute(cross, "gy", cross_to)
 
-    strip, group = 16, 4
+    strip, group, chunk, last = 16, 2, xs // 4, xs // 2
     big = shape((xs, ys, cols), bf16)
-    updated, residual, strips = call(
-        functools.partial(update_body, strip, group),
-        (big, big, shape((2, xs, strip, cols), f32)),
+    updated, residual, strips, late = call(
+        functools.partial(update_body, strip, group, chunk, last),
+        (
+            big,
+            big,
+            shape((2, xs, strip, cols), f32),
+            shape((last, ys - 2 * strip, cols), bf16),
+        ),
         [VMEM] * 6,
-        out_specs=(ANY, ANY, VMEM),
+        out_specs=(ANY, ANY, VMEM, VMEM),
         scratch=[
             pltpu.VMEM((xs + 2, ys, cols), bf16),
             pltpu.VMEM((xs, ys - 2 * strip, cols), bf16),
-            pltpu.SemaphoreType.DMA((2,)),
+            pltpu.SemaphoreType.DMA((2 * xs // chunk,)),
         ],
         cost=(20 * xs * ys * cols, 10 << 20),
     )(part, waves, halo, kerr_b, wave_b, source)
 
     residual = call(
-        functools.partial(seam_body, n_gy, strip),
+        functools.partial(seam_body, n_gy, strip, last),
         big,
-        [VMEM, VMEM, VMEM, ANY],
+        [VMEM] * 4 + [ANY],
         out_specs=ANY,
         scratch=[
             pltpu.VMEM((2, xs * strip, cols), f32),
             pltpu.VMEM((2, xs, strip, cols), bf16),
-            pltpu.SemaphoreType.DMA((2,)),
+            pltpu.SemaphoreType.DMA((3,)),
         ],
-        aliases={3: 0},
-    )(strips, pair, cross, residual)
+        aliases={4: 0},
+    )(strips, late, pair, cross, residual)
     return updated, residual
 
 

time: 20.6 us -> 18 us (0.87)
  Pallas kernels: 10.2 us -> 7.59 us
    pallas_call x7, Pallas kernels: 10.2 us -> 7.59 us  [run(): pl.pallas_call(body, out_shape=outs, in_specs=ins, out_specs=out_specs if...]
  transfers between devices with their start and end apart: 4 -> 4, of which waited for: 2 -> 2; matrix products, arithmetic and copies ran while one was open for 0% -> 0% of each run, Pallas kernels for 32% -> 23%
where the time goes in v3:
time: 18 us; the launch traced here: 17.9 us
  starting transfers between devices  8.14 us (45%)
  Pallas kernels  7.59 us (42%)
  waiting for transfers between devices  1.37 us (8%)
  between operations  0.74 us (4%)
    pallas_call x7, Pallas kernels, run(): pl.pallas_call(body, out_shape=outs, in_specs=ins, out_specs=out_specs if...  7.59 us
    ppermute x1, starting transfers between devices, per_device(): other = lax.ppermute(message, 'gx', [(i, i ^ 1) for i in range(n_gx)])  3.09 us
    ppermute x1, starting transfers between devices, per_device(): far = lax.ppermute(reach, 'gx', [(i, i ^ 2) for i in range(n_gx)])  3.05 us
    ppermute x1, starting transfers between devices, per_device(): cross = lax.ppermute(cross, 'gy', cross_to)  1.94 us
    ppermute x1, waiting for transfers between devices, per_device(): other = lax.ppermute(message, 'gx', [(i, i ^ 1) for i in range(n_gx)])  0.78 us
    ppermute x1, waiting for transfers between devices, per_device(): far = lax.ppermute(reach, 'gx', [(i, i ^ 2) for i in range(n_gx)])  0.58 us
  transfers between devices with their start and end apart: 4, of which 2 were waited for; matrix products, arithmetic and copies ran while one was open for 0% of the time, Pallas kernels for 23%

profile of v3, /device:TPU:0, one launch (start us, length us, event | category | flops | bytes accessed | tf_op | source)
XLA Modules:
  0.0 17.9 jit_solution(17525741610498290850)
XLA Ops:
  0.6 0.0 copy-start.1
  0.6 0.0 copy-start.3
  0.7 0.0 copy-start.2
  0.7 0.0 copy-start
  0.7 2.2 %shard_map.77 = (bf16[160,128]{1,0:T(8,128)(2,1)S(1)}, bf16[2,16,64,128]{3,2,1,0:T(8,128)(2,1)S(1)}) custom-call(bf16[64,64,128]{2,1,0:T(8,128)(2,1)} %source.3, bf16[64,64,128]{2,1,0:T(8,128)(2,1)} %field.2, f32[64,64]{1,0:T(8,128)} %kerr.1, bf16[4,4,256,256]{3,2,1,0:T(8,128)(2,1)} %leaf_ops.2, f32[1,64,64]{2,1,0:T(8,128)} %transfer.1), custom_call_target="tpu_custom_call" | custom-call | flops 33554432 | bytes 2097152 | tf_op jit(solution)/shard_map/pallas_call | solution.py:19
  2.9 0.0 copy-start.4
  2.9 3.1 %collective-permute-start = (bf16[160,128]{1,0:T(8,128)(2,1)S(1)}, bf16[160,128]{1,0:T(8,128)(2,1)S(1)}, u32[]{:S(2)}, u32[]{:S(2)}) collective-permute-start(bf16[160,128]{1,0:T(8,128)(2,1)S(1)} %get-tuple-element.34.own), channel_id=1, source_target_pairs={{0,4},{4,0},{8,12},{12,8},{1,5},{5,1},{9,13},{13,9},{2,6},{6,2},{1... | collective-permute-start | bytes 122888 | tf_op jit(solution)/shard_map/ppermute | solution.py:352
  6.0 0.0 copy-done.1
  6.0 0.0 copy-done.3
  6.0 0.0 copy-done.2
  6.0 0.0 copy-done
  6.0 1.2 %shard_map.78 = (f32[4096,128]{1,0:T(8,128)S(1)}, f32[128,128]{1,0:T(8,128)S(1)}) custom-call(bf16[2,16,64,128]{3,2,1,0:T(8,128)(2,1)S(1)} %get-tuple-element.35.edge, bf16[64,64,128]{2,1,0:T(8,128)(2,1)S(1)} %copy-done, bf16[64,64,128]{2,1,0:T(8,128)(2,1)S(1)} %copy-done.2, f32[64,64]{1,0:T(8,128)S(1)} %copy-done.3, bf16[4,4,256,256]{3,2,1,0:T(8,128)(2,1)S(1)} %copy-done.1), custom_call_target="tpu_custom_call" | custom-call | flops 268435456 | bytes 6291456 | tf_op jit(solution)/shard_map/pallas_call | solution.py:19
  7.2 0.8 %collective-permute-done.got = bf16[160,128]{1,0:T(8,128)(2,1)S(1)} collective-permute-done((bf16[160,128]{1,0:T(8,128)(2,1)S(1)}, bf16[160,128]{1,0:T(8,128)(2,1)S(1)}, u32[]{:S(2)}, u32[]{:S(2)}) %collective-permute-start) | collective-permute-done | bytes 40992 | tf_op jit(solution)/shard_map/ppermute | solution.py:352
  8.0 0.2 %shard_map.79 = (bf16[128,128]{1,0:T(8,128)(2,1)S(1)}, f32[3,64,128]{2,1,0:T(8,128)S(1)}, bf16[64,64]{1,0:T(8,128)(2,1)S(1)}) custom-call(bf16[160,128]{1,0:T(8,128)(2,1)S(1)} %get-tuple-element.34.own, bf16[160,128]{1,0:T(8,128)(2,1)S(1)} %collective-permute-done.got), custom_call_target="tpu_custom_call" | custom-call | tf_op jit(solution)/shard_map/pallas_call | solution.py:19
  8.2 3.0 %collective-permute-start.1 = (bf16[128,128]{1,0:T(8,128)(2,1)S(1)}, bf16[128,128]{1,0:T(8,128)(2,1)S(1)}, u32[]{:S(2)}, u32[]{:S(2)}) collective-permute-start(bf16[128,128]{1,0:T(8,128)(2,1)S(1)} %get-tuple-element.44), channel_id=1, source_target_pairs={{0,8},{4,12},{8,0},{12,4},{1,9},{5,13},{9,1},{13,5},{2,10},{6,14},... | collective-permute-start | bytes 98312 | tf_op jit(solution)/shard_map/ppermute | solution.py:377
  11.2 0.0 copy-done.4
  11.2 1.3 %shard_map.80 = (f32[64,64,128]{2,1,0:T(8,128)S(1)}, f32[64,64,128]{2,1,0:T(8,128)S(1)}) custom-call(f32[64,64]{1,0:T(8,128)S(1)} %copy-done.3, f32[64,64]{1,0:T(8,128)S(1)} %copy-done.4), custom_call_target="tpu_custom_call" | custom-call | flops 524288 | bytes 4194304 | tf_op jit(solution)/shard_map/pallas_call | solution.py:19
  12.6 0.6 %collective-permute-done.1.got = bf16[128,128]{1,0:T(8,128)(2,1)S(1)} collective-permute-done((bf16[128,128]{1,0:T(8,128)(2,1)S(1)}, bf16[128,128]{1,0:T(8,128)(2,1)S(1)}, u32[]{:S(2)}, u32[]{:S(2)}) %collective-permute-start.1) | collective-permute-done | bytes 32800 | tf_op jit(solution)/shard_map/ppermute | solution.py:377
  13.1 0.2 %shard_map.81 = (f32[2,64,128]{2,1,0:T(8,128)S(1)}, bf16[2,64,128]{2,1,0:T(8,128)(2,1)S(1)}, bf16[64,128]{1,0:T(8,128)(2,1)S(1)}, bf16[64,128]{1,0:T(8,128)(2,1)S(1)}) custom-call(bf16[128,128]{1,0:T(8,128)(2,1)S(1)} %collective-permute-done.1.got, f32[3,64,128]{2,1,0:T(8,128)S(1)} %get-tuple-element.49.keep, ...), custom_call_target="tpu_custom_call" | custom-call | tf_op jit(solution)/shard_map/pallas_call | solution.py:19
  13.3 0.1 collective-permute-start.2
  13.4 1.9 %collective-permute-start.3 = (bf16[64,128]{1,0:T(8,128)(2,1)S(1)}, bf16[64,128]{1,0:T(8,128)(2,1)S(1)}, u32[]{:S(2)}, u32[]{:S(2)}) collective-permute-start(bf16[64,128]{1,0:T(8,128)(2,1)S(1)} %get-tuple-element.60), channel_id=1, source_target_pairs={{0,3},{1,2},{2,1},{3,0},{4,7},{5,6},{6,5},{7,4},{8,11},{9,10},{10,... | collective-permute-start | bytes 49160 | tf_op jit(solution)/shard_map/ppermute | solution.py:391
  15.4 1.6 %shard_map.82 = (bf16[64,64,128]{2,1,0:T(8,128)(2,1)}, bf16[64,64,128]{2,1,0:T(8,128)(2,1)}, f32[2,64,16,128]{3,2,1,0:T(8,128)S(1)}, bf16[32,32,128]{2,1,0:T(8,128)(2,1)S(1)}) custom-call(f32[4096,128]{1,0:T(8,128)S(1)} %get-tuple-element.42.part, f32[2,64,128]{2,1,0:T(8,128)S(1)} %get-tuple-element.52.waves, ...), custom_call_target="tpu_custom_call" | custom-call | flops 10485760 | bytes 10485760 | tf_op jit(solution)/shard_map/pallas_call | solution.py:19
  16.9 0.0 collective-permute-done.2.pair
  16.9 0.0 collective-permute-done.3.cross
  17.0 0.9 %shard_map.83 = bf16[64,64,128]{2,1,0:T(8,128)(2,1)} custom-call(f32[2,64,16,128]{3,2,1,0:T(8,128)S(1)} %get-tuple-element.57.strips, bf16[32,32,128]{2,1,0:T(8,128)(2,1)S(1)} %get-tuple-element.58.late, bf16[64,128]{1,0:T(8,128)(2,1)S(1)} %collective-permute-done.2.pair, ...), custom_call_target="tpu_custom_call", output_to_operand_aliasing={{}: (4, {})} | custom-call | tf_op jit(solution)/shard_map/pallas_call | solution.py:19
Async XLA Ops:
  0.6 5.4 %copy-start.1 = (bf16[4,4,256,256]{3,2,1,0:T(8,128)(2,1)S(1)}, bf16[4,4,256,256]{3,2,1,0:T(8,128)(2,1)}, u32[]{:S(2)}) copy-start(bf16[4,4,256,256]{3,2,1,0:T(8,128)(2,1)} %leaf_ops.2) | copy-start | bytes 6291460
  0.6 5.4 %copy-start.3 = (f32[64,64]{1,0:T(8,128)S(1)}, f32[64,64]{1,0:T(8,128)}, u32[]{:S(2)}) copy-start(f32[64,64]{1,0:T(8,128)} %kerr.1) | copy-start | bytes 49156
  0.7 5.4 %copy-start.2 = (bf16[64,64,128]{2,1,0:T(8,128)(2,1)S(1)}, bf16[64,64,128]{2,1,0:T(8,128)(2,1)}, u32[]{:S(2)}) copy-start(bf16[64,64,128]{2,1,0:T(8,128)(2,1)} %field.2) | copy-start | bytes 3145732
  0.7 5.4 %copy-start = (bf16[64,64,128]{2,1,0:T(8,128)(2,1)S(1)}, bf16[64,64,128]{2,1,0:T(8,128)(2,1)}, u32[]{:S(2)}) copy-start(bf16[64,64,128]{2,1,0:T(8,128)(2,1)} %source.3) | copy-start | bytes 3145732
  2.9 8.3 %copy-start.4 = (f32[64,64]{1,0:T(8,128)S(1)}, f32[64,64]{1,0:T(8,128)}, u32[]{:S(2)}) copy-start(f32[64,64]{1,0:T(8,128)} %wave) | copy-start | bytes 49156
  2.9 5.1 %collective-permute-start = (bf16[160,128]{1,0:T(8,128)(2,1)S(1)}, bf16[160,128]{1,0:T(8,128)(2,1)S(1)}, u32[]{:S(2)}, u32[]{:S(2)}) collective-permute-start(bf16[160,128]{1,0:T(8,128)(2,1)S(1)} %get-tuple-element.34.own), channel_id=1, source_target_pairs={{0,4},{4,0},{8,12},{12,8},{1,5},{5,1},{9,13},{13,9},{2,6},{6,2},{1... | collective-permute-start | bytes 122888 | tf_op jit(solution)/shard_map/ppermute | solution.py:352
  8.2 4.9 %collective-permute-start.1 = (bf16[128,128]{1,0:T(8,128)(2,1)S(1)}, bf16[128,128]{1,0:T(8,128)(2,1)S(1)}, u32[]{:S(2)}, u32[]{:S(2)}) collective-permute-start(bf16[128,128]{1,0:T(8,128)(2,1)S(1)} %get-tuple-element.44), channel_id=1, source_target_pairs={{0,8},{4,12},{8,0},{12,4},{1,9},{5,13},{9,1},{13,5},{2,10},{6,14},... | collective-permute-start | bytes 98312 | tf_op jit(solution)/shard_map/ppermute | solution.py:377
  13.3 3.6 %collective-permute-start.2 = (bf16[64,128]{1,0:T(8,128)(2,1)S(1)}, bf16[64,128]{1,0:T(8,128)(2,1)S(1)}, u32[]{:S(2)}, u32[]{:S(2)}) collective-permute-start(bf16[64,128]{1,0:T(8,128)(2,1)S(1)} %get-tuple-element.59), channel_id=1, source_target_pairs={{0,1},{1,0},{2,3},{3,2},{4,5},{5,4},{6,7},{7,6},{8,9},{9,8},{10,11... | collective-permute-start | bytes 49160 | tf_op jit(solution)/shard_map/ppermute | solution.py:390
  13.4 3.5 %collective-permute-start.3 = (bf16[64,128]{1,0:T(8,128)(2,1)S(1)}, bf16[64,128]{1,0:T(8,128)(2,1)S(1)}, u32[]{:S(2)}, u32[]{:S(2)}) collective-permute-start(bf16[64,128]{1,0:T(8,128)(2,1)S(1)} %get-tuple-element.60), channel_id=1, source_target_pairs={{0,3},{1,2},{2,1},{3,0},{4,7},{5,6},{6,5},{7,4},{8,11},{9,10},{10,... | collective-permute-start | bytes 49160 | tf_op jit(solution)/shard_map/ppermute | solution.py:391

commit v4 on v3

--- a/solution.py
+++ b/solution.py
@@ -45,8 +45,15 @@
     return (s - kerr * f * f * f).astype(bf16)
 
 
+def seat(paired):
+    if not paired:
+        return True, True
+    place = lax.axis_index("gx")
+    return place < 2, (place == 1) | (place == 2)
+
+
 def faces_body(
-    half, points, parts, source, field, kerr_all, leaf_ops, transfer, msg, edge, src, fld, ops,
+    paired, points, parts, source, field, kerr_all, leaf_ops, transfer, far, near, edge, src, fld, ops,
     kerr, own, kb, sems, more,
 ):
     lx, ly, pts, _ = leaf_ops.shape
@@ -72,7 +79,7 @@
         rows_of[e].start()
     matrix = copy(transfer.at[0], own, more.at[1])
     matrix.start()
-    is_a = lax.axis_index("gx") < half
+    is_a, inner = seat(paired)
     coef.wait()
     kts = [kerr[x0 : x0 + points, :].T for x0 in firsts]
     for e in range(2):
@@ -92,59 +99,57 @@
             rows.append(matmul(ops[e, b], rhs))
         faces.append(jnp.concatenate(rows, axis=0).astype(bf16))
     left, right = faces
-    msg[0:ys, :] = jnp.where(is_a, right, left)
-    msg[ys : 2 * ys, :] = jnp.where(is_a, left, right)
+    toward = jnp.where(is_a, right, left)
+    far[0:ys, :] = toward
+    near[0:ys, :] = jnp.where(inner, jnp.where(is_a, left, right), toward)
     matrix.wait()
     x_map = jnp.where(is_a, own[...], own[...].T).astype(bf16)
-    msg[2 * ys :, :] = jnp.concatenate([x_map[: ys // 2], x_map[ys // 2 :]], axis=1)
-
-
-def split_message(m, ys):
-    packed = m[2 * ys :]
-    return m[:ys], m[ys : 2 * ys], jnp.concatenate([packed[:, :ys], packed[:, ys:]], axis=0)
-
-
-def leaves_body(points, edge, source, field, kerr, leaf_ops, part, ends, rhs_all):
+    x_map = jnp.concatenate([x_map[: ys // 2], x_map[ys // 2 :]], axis=1)
+    far[ys:, :] = x_map
+    near[ys:, :] = x_map
+
+
+def unpack(message):
+    cols = message.shape[1]
+    ys = 2 * message.shape[0] // 3
+    packed = message[ys:]
+    half = cols // 2
+    return message[:ys], jnp.concatenate([packed[:, :half], packed[:, half:]], axis=0)
+
+
+def leaves_body(
+    points, edge, source, field, kerr, leaf_ops, part, ends, mid, fld, rhs_all, sems
+):
     lx, ly, pts, _ = leaf_ops.shape
     xs, ys, cols = source.shape
-    kt = kerr[...].T
-    for a in range(lx):
-        for q in range(points):
-            x = a * points + q
-            if a == 0:
-                col = edge[0, q]
-            elif a == lx - 1:
-                col = edge[1, q]
-            else:
-                col = kerr_column(source[x], field[x], kt[:, x : x + 1])
-            rhs_all[x] = col
+    inner = pl.ds(points, xs - 2 * points)
+    copies = [
+        pltpu.make_async_copy(source.at[inner], mid, sems.at[0]),
+        pltpu.make_async_copy(field.at[inner], fld, sems.at[1]),
+    ]
+    for c in copies:
+        c.start()
+
+    def leaf_row(a, rows):
         for b in range(ly):
-            rhs = rhs_all[a * points : (a + 1) * points, b * points : (b + 1) * points, :]
-            out = matmul(leaf_ops[a, b], rhs.reshape(pts, cols))
+            rhs = rows[:, b * points : (b + 1) * points, :].reshape(pts, cols)
+            out = matmul(leaf_ops[a, b], rhs)
             for q in range(points):
                 r = (a * points + q) * ys + b * points
                 part[r : r + points, :] = out[q * points : (q + 1) * points, :]
+
+    leaf_row(0, edge.at[0])
+    leaf_row(lx - 1, edge.at[1])
+    kt = kerr[...].T
+    for c in copies:
+        c.wait()
+    for a in range(1, lx - 1):
+        for q in range(points):
+            x, r = a * points + q, (a - 1) * points + q
+            rhs_all[r] = kerr_column(mid[r], fld[r], kt[:, x : x + 1])
+        leaf_row(a, rhs_all.at[pl.ds((a - 1) * points, points)])
     ends[0:xs, :] = part[pl.ds(0, xs, stride=ys), :]
     ends[xs:, :] = part[pl.ds(ys - 1, xs, stride=ys), :]
-
-
-def compose_body(count, xs, own, got, msg, keep, inner_map):
-    ys = own.shape[1] // 2
-    place = lax.axis_index("gx")
-    inner = (place == count // 2 - 1) | (place == count // 2)
-    f_own, g_own, x_own = split_message(own[...], ys)
-    f_got, g_got, x_got = split_message(got[...], ys)
-    f_in = jnp.where(inner, f_own, f_got)
-    g_in = jnp.where(inner, g_own, g_got)
-    x_in = jnp.where(inner, x_own, x_got)
-    f_out = jnp.where(inner, f_got, f_own)
-    reach = matmul(x_in, f_out) + f_in.astype(f32)
-    msg[0:ys, :] = reach.astype(bf16)
-    msg[ys:, :] = (f_in.astype(f32) + (lift_weight / xs) * f_out.astype(f32)).astype(bf16)
-    keep[0] = f_out.astype(f32)
-    keep[1] = g_in.astype(f32)
-    keep[2] = reach
-    inner_map[...] = x_in
 
 
 def weights_body(kerr, wave, kerr_b, wave_b):
@@ -171,34 +176,41 @@
     cross[...] = jnp.where(even, low, high).astype(bf16)
 
 
-def finish_body(count, got, keep, inner_map, ends, waves, halo, pair, cross):
-    ys = got.shape[0] // 2
+def finish_body(far, near, got_1, got_2, got_3, ends, waves, halo, pair, cross):
     xs = pair.shape[0]
-    place = lax.axis_index("gx")
-    inner = (place == count // 2 - 1) | (place == count // 2)
-    is_a = place < count // 2
-    back = got[0:ys, :]
-    e_got = got[ys:, :].astype(f32)
-    f_out, g_in, reach = keep[0], keep[1], keep[2]
-    t = lax.dot_general(
-        inner_map[...], back, (((0,), (0,)), ((), ())), preferred_element_type=f32
-    ) + g_in
-    back = back.astype(f32)
-    forward = jnp.where(inner, f_out, 0.0)
-    backward = jnp.where(inner, back, t)
-    w = lift_weight * jnp.where(is_a, forward, backward)
-    z = lift_weight * jnp.where(is_a, backward, forward)
+    is_a, inner = seat(True)
+    own_face, own_map = unpack(far[...])
+    own_near, _ = unpack(near[...])
+    mate_face, mate_map = unpack(got_1[...])
+    face_2, map_2 = unpack(got_2[...])
+    face_3, map_3 = unpack(got_3[...])
+    other_map = jnp.where(inner, map_3, map_2)
+    other_in = jnp.where(inner, face_3, face_2).astype(f32)
+    other_out = jnp.where(inner, face_2, face_3)
+    back_in = matmul(other_map, other_out) + other_in
+    in_map = jnp.where(inner, own_map, mate_map)
+    out_face = jnp.where(inner, mate_face, own_face)
+    in_back = jnp.where(inner, own_near, mate_face).astype(f32)
+    reach = matmul(in_map, out_face) + own_face.astype(f32)
+    back_out = in_back + lax.dot_general(
+        in_map, back_in.astype(bf16), (((0,), (0,)), ((), ())), preferred_element_type=f32
+    )
+    out_face, other_out = out_face.astype(f32), other_out.astype(f32)
+    ahead = jnp.where(inner, out_face, 0.0)
+    back = jnp.where(inner, back_in, back_out)
+    w = lift_weight * jnp.where(is_a, ahead, back)
+    z = lift_weight * jnp.where(is_a, back, ahead)
     waves[0] = w
     waves[1] = z
+    edge_columns(ends, w, z, pair, cross)
     toward = jnp.where(
         inner,
-        e_got + lift_weight * reach,
-        g_in + lift_weight * (f_out + back * (1.0 / xs)),
+        other_in + lift_weight * (reach + other_out * (1.0 / xs)),
+        in_back + lift_weight * (out_face + back_in * (1.0 / xs)),
     )
-    away = jnp.where(inner, f_out + lift_weight * t, 0.0)
+    away = jnp.where(inner, out_face + lift_weight * back_out, 0.0)
     halo[0] = jnp.where(is_a, away, toward).astype(bf16)
     halo[1] = jnp.where(is_a, toward, away).astype(bf16)
-    edge_columns(ends, w, z, pair, cross)
 
 
 def ends_body(ends, waves, pair, cross):
@@ -214,10 +226,17 @@
 
 
 def update_body(
-    strip, group, chunk, last, part, waves, halo, kerr_b, wave_b, source, updated, residual,
+    strip, group, chunk, last, part, waves, halo, kerr_b, wave_b, src, mid, updated, residual,
     strips, late, u, res, sems,
 ):
-    xs, ys, cols = source.shape
+    xs, ys, cols = updated.shape
+    points = src.shape[1]
+
+    def source(x):
+        if x < points:
+            return src[0, x]
+        return src[1, x - xs + points] if x >= xs - points else mid[x - points]
+
     w, z = waves[0], waves[1]
     u[0] = halo[0]
     u[xs + 1] = halo[1]
@@ -229,9 +248,8 @@
         copies.append(pltpu.make_async_copy(src, dst, sems.at[len(copies)]))
         copies[-1].start()
 
-    def lift(x):
-        lp, rp = (xs - x) / xs, (x + 1) / xs
-        u[x + 1] = (part[x * ys : (x + 1) * ys, :] + (lp * w + rp * z)).astype(bf16)
+    def lift(x, rise):
+        u[x + 1] = (part[x * ys : (x + 1) * ys, :] + rise).astype(bf16)
         if (x + 1) % chunk == 0:
             at = pl.ds(x + 1 - chunk, chunk)
             send(u.at[pl.ds(x + 2 - chunk, chunk)], updated.at[at])
@@ -240,7 +258,7 @@
         near = matmul(taps, u[x : x + group + 2].reshape((group + 2) * ys, cols))
         for q in range(group):
             m = u[x + q + 1].astype(f32)
-            s = source[x + q].astype(f32)
+            s = source(x + q).astype(f32)
             r = near[q * ys : (q + 1) * ys] + (m * (wave_b[x + q] + kerr_b[x + q] * (m * m)) - s)
             strips[0, x + q] = r[:strip, :]
             strips[1, x + q] = r[ys - strip :, :]
@@ -255,9 +273,11 @@
             send(res.at[at], residual.at[at, inside])
 
     ahead = 64
+    rise, slope = w + z * (1.0 / xs), (z - w) * (1.0 / xs)
     for x in range(xs + ahead):
         if x < xs:
-            lift(x)
+            lift(x, rise)
+            rise = rise + slope
         if x >= ahead and (x - ahead) % group == 0:
             residue(x - ahead)
     for c in copies:
@@ -294,12 +314,12 @@
         c.wait()
 
 
-def gathered_sweeps(message, ys, xs, count):
+def gathered_sweeps(far, near, ys, xs, count):
     place = lax.axis_index("gx")
-    every = lax.all_gather(message, "gx").astype(f32)
-    right, left = every[:, :ys], every[:, ys : 2 * ys]
-    packed = every[:, 2 * ys :]
-    maps = jnp.concatenate([packed[:, :, :ys], packed[:, :, ys:]], axis=1)
+    every, left = (lax.all_gather(m, "gx").astype(f32) for m in (far, near))
+    right, left = every[:, :ys], left[:, :ys]
+    half = every.shape[2] // 2
+    maps = jnp.concatenate([every[:, ys:, :half], every[:, ys:, half:]], axis=1)
     start = jnp.zeros_like(right[0])
     exact = functools.partial(jnp.dot, precision=lax.Precision.HIGHEST)
 
@@ -324,40 +344,48 @@
     lx, ly, pts, _ = leaf_ops.shape
     points = xs // lx
     n_gx, n_gy = lax.axis_size("gx"), lax.axis_size("gy")
-    doubling = n_gx == 4
+    paired = n_gx == 4
     shape = jax.ShapeDtypeStruct
     dots = 2 * lx * ly * pts * pts * cols
 
-    message, edge = call(
-        functools.partial(faces_body, n_gx // 2 if doubling else n_gx, points, 1),
-        (shape((2 * ys + ys // 2, cols), bf16), shape((2, points, ys, cols), bf16)),
+    edges = shape((2, points, ys, cols), bf16)
+    edges = shape((2, points, ys, cols), bf16)
+    message = shape((ys + ys // 2, cols), bf16)
+    far, near, edge, src = call(
+        functools.partial(faces_body, paired, points, 1),
+        (message, message, edges, edges),
         [HBM] * 5,
         scratch=[
-            pltpu.VMEM((2, points, ys, cols), bf16),
             pltpu.VMEM((2, points, ys, cols), bf16),
             pltpu.VMEM((2, ly, points, pts), bf16),
             pltpu.VMEM((xs, ys), f32),
             pltpu.VMEM((ys, ys), f32),
             pltpu.VMEM((2, points, ys, cols), f32),
-            pltpu.SemaphoreType.DMA((2, 8)),
+            pltpu.SemaphoreType.DMA((2, 2)),
             pltpu.SemaphoreType.DMA((4,)),
         ],
         cost=(dots // 8, 2 << 20),
     )(*map(in_hbm, (source, field, kerr, leaf_ops, transfer_ops)))
-    message, edge, source, field, kerr, wave, leaf_ops = lax.optimization_barrier(
-        (message, edge, source, field, kerr, wave, leaf_ops)
+    far, near, edge, source, field, kerr, wave, leaf_ops = lax.optimization_barrier(
+        (far, near, edge, source, field, kerr, wave, leaf_ops)
     )
 
-    if doubling:
-        other = lax.ppermute(message, "gx", [(i, i ^ 1) for i in range(n_gx)])
-
-    part, ends = call(
+    if paired:
+        sent = [(2, far), (3, far), (1, near)]
+        got = [lax.ppermute(m, "gx", [(i, i ^ k) for i in range(n_gx)]) for k, m in sent]
+
+    between = shape((xs - 2 * points, ys, cols), bf16)
+    part, ends, mid = call(
         functools.partial(leaves_body, points),
-        (shape((xs * ys, cols), f32), shape((2 * xs, cols), f32)),
-        [VMEM] * 5,
-        scratch=[pltpu.VMEM((xs, ys, cols), bf16)],
+        (shape((xs * ys, cols), f32), shape((2 * xs, cols), f32), between),
+        [VMEM, HBM, HBM, VMEM, VMEM],
+        scratch=[
+            pltpu.VMEM(between.shape, bf16),
+            pltpu.VMEM(between.shape, bf16),
+            pltpu.SemaphoreType.DMA((2,)),
+        ],
         cost=(dots, 6 << 20),
-    )(edge, source, field, kerr, leaf_ops)
+    )(edge, in_hbm(source), in_hbm(field), kerr, leaf_ops)
 
     kerr_b, wave_b = call(
         weights_body,
@@ -367,22 +395,17 @@
     )(kerr, wave)
 
     column = shape((xs, cols), bf16)
-    if doubling:
-        other, part, ends = lax.optimization_barrier((other, part, ends))
-        reach, keep, inner_map = call(
-            functools.partial(compose_body, n_gx, xs),
-            (shape((2 * ys, cols), bf16), shape((3, ys, cols), f32), shape((ys, ys), bf16)),
-            [VMEM] * 2,
-        )(message, other)
-        far = lax.ppermute(reach, "gx", [(i, i ^ 2) for i in range(n_gx)])
-        far, kerr_b, wave_b = lax.optimization_barrier((far, kerr_b, wave_b))
+    if paired:
+        *got, part, ends, kerr_b, wave_b = lax.optimization_barrier(
+            (*got, part, ends, kerr_b, wave_b)
+        )
         waves, halo, pair, cross = call(
-            functools.partial(finish_body, n_gx),
+            finish_body,
             (shape((2, ys, cols), f32), shape((2, ys, cols), bf16), column, column),
-            [VMEM] * 4,
-        )(far, keep, inner_map, ends)
+            [VMEM] * 6,
+        )(far, near, got[2], got[0], got[1], ends)
     else:
-        waves, halo = gathered_sweeps(message, ys, xs, n_gx)
+        waves, halo = gathered_sweeps(far, near, ys, xs, n_gx)
         pair, cross = call(ends_body, (column, column), [VMEM] * 2)(ends, waves)
 
     pair_to = [(i, i + 1 - 2 * (i % 2)) for i in range(n_gy)]
@@ -400,7 +423,7 @@
             shape((2, xs, strip, cols), f32),
             shape((last, ys - 2 * strip, cols), bf16),
         ),
-        [VMEM] * 6,
+        [VMEM] * 7,
         out_specs=(ANY, ANY, VMEM, VMEM),
         scratch=[
             pltpu.VMEM((xs + 2, ys, cols), bf16),
@@ -408,7 +431,7 @@
             pltpu.SemaphoreType.DMA((2 * xs // chunk,)),
         ],
         cost=(20 * xs * ys * cols, 10 << 20),
-    )(part, waves, halo, kerr_b, wave_b, source)
+    )(part, waves, halo, kerr_b, wave_b, src, mid)
 
     residual = call(
         functools.partial(seam_body, n_gy, strip, last),

time: 18 us -> 17.3 us (0.961)
  starting transfers between devices: 8.14 us -> 7.43 us
  Pallas kernels: 7.59 us -> 8.15 us
  waiting for transfers between devices: 1.37 us -> 0.86 us
    ppermute x2 -> x3, waiting for transfers between devices: 1.36 us -> 0.69 us  [per_device(): lax.ppermute(m, 'gx', [(i, i ^ k) for i in range(n_gx)])]
    pallas_call x7 -> x6, Pallas kernels: 7.59 us -> 8.15 us  [run(): pl.pallas_call(body, out_shape=outs, in_specs=ins, out_specs=out_specs if...]
    ppermute x2 -> x3, starting transfers between devices: 6.14 us -> 5.76 us  [per_device(): lax.ppermute(m, 'gx', [(i, i ^ k) for i in range(n_gx)])]
    ppermute x1, starting transfers between devices: 1.94 us -> 1.61 us  [per_device(): cross = lax.ppermute(cross, 'gy', cross_to)]
  transfers between devices with their start and end apart: 4 -> 5, of which waited for: 2 -> 2; matrix products, arithmetic and copies ran while one was open for 0% -> 0% of each run, Pallas kernels for 23% -> 28%
where the time goes in v4:
time: 17.3 us; the launch traced here: 17.2 us
  Pallas kernels  8.15 us (47%)
  starting transfers between devices  7.43 us (43%)
  waiting for transfers between devices  0.86 us (5%)
  between operations  0.73 us (4%)
    pallas_call x6, Pallas kernels, run(): pl.pallas_call(body, out_shape=outs, in_specs=ins, out_specs=out_specs if...  8.15 us
    ppermute x3, starting transfers between devices, per_device(): lax.ppermute(m, 'gx', [(i, i ^ k) for i in range(n_gx)])  5.76 us
    ppermute x1, starting transfers between devices, per_device(): cross = lax.ppermute(cross, 'gy', cross_to)  1.61 us
    ppermute x3, waiting for transfers between devices, per_device(): lax.ppermute(m, 'gx', [(i, i ^ k) for i in range(n_gx)])  0.69 us
  transfers between devices with their start and end apart: 5, of which 2 were waited for; matrix products, arithmetic and copies ran while one was open for 0% of the time, Pallas kernels for 28%

profile of v4, /device:TPU:0, one launch (start us, length us, event | category | flops | bytes accessed | tf_op | source)
XLA Modules:
  0.0 17.2 jit_solution(6369747563985939870)
XLA Ops:
  0.6 0.0 copy-start
  0.6 0.0 copy-start.1
  0.7 0.0 copy-start.2
  0.7 2.1 %shard_map.77 = (bf16[96,128]{1,0:T(8,128)(2,1)S(1)}, bf16[96,128]{1,0:T(8,128)(2,1)S(1)}, bf16[2,16,64,128]{3,2,1,0:T(8,128)(2,1)S(1)}, bf16[2,16,64,128]{3,2,1,0:T(8,128)(2,1)S(1)}) custom-call(bf16[64,64,128]{2,1,0:T(8,128)(2,1)} %source.2, bf16[64,64,128]{2,1,0:T(8,128)(2,1)} %field.2, f32[64,64]{1,0:T(8,128)} %kerr.1, ...), custom_call_target="tpu_custom_call" | custom-call | flops 33554432 | bytes 2097152 | tf_op jit(solution)/shard_map/pallas_call | solution.py:19
  2.8 5.1 %collective-permute-start.1 = (bf16[96,128]{1,0:T(8,128)(2,1)S(1)}, bf16[96,128]{1,0:T(8,128)(2,1)S(1)}, u32[]{:S(2)}, u32[]{:S(2)}) collective-permute-start(bf16[96,128]{1,0:T(8,128)(2,1)S(1)} %get-tuple-element.37.far), channel_id=1, source_target_pairs={{0,12},{4,8},{8,4},{12,0},{1,13},{5,9},{9,5},{13,1},{2,14},{6,10},... | collective-permute-start | bytes 73736 | tf_op jit(solution)/shard_map/ppermute | solution.py:375
  7.9 0.0 collective-permute-start
  7.9 0.6 %collective-permute-start.2 = (bf16[96,128]{1,0:T(8,128)(2,1)S(1)}, bf16[96,128]{1,0:T(8,128)(2,1)S(1)}, u32[]{:S(2)}, u32[]{:S(2)}) collective-permute-start(bf16[96,128]{1,0:T(8,128)(2,1)S(1)} %get-tuple-element.38.near), channel_id=1, source_target_pairs={{0,4},{4,0},{8,12},{12,8},{1,5},{5,1},{9,13},{13,9},{2,6},{6,2},{1... | collective-permute-start | bytes 73736 | tf_op jit(solution)/shard_map/ppermute | solution.py:375
  8.6 0.0 copy-done.1
  8.6 0.0 copy-done.2
  8.6 1.3 %shard_map.79 = (f32[64,64,128]{2,1,0:T(8,128)S(1)}, f32[64,64,128]{2,1,0:T(8,128)S(1)}) custom-call(f32[64,64]{1,0:T(8,128)S(1)} %copy-done.1, f32[64,64]{1,0:T(8,128)S(1)} %copy-done.2), custom_call_target="tpu_custom_call" | custom-call | flops 524288 | bytes 4194304 | tf_op jit(solution)/shard_map/pallas_call | solution.py:19
  9.9 0.0 copy-done
  9.9 2.0 %shard_map.78 = (f32[4096,128]{1,0:T(8,128)S(1)}, f32[128,128]{1,0:T(8,128)S(1)}, bf16[32,64,128]{2,1,0:T(8,128)(2,1)S(1)}) custom-call(bf16[2,16,64,128]{3,2,1,0:T(8,128)(2,1)S(1)} %get-tuple-element.39.edge, bf16[64,64,128]{2,1,0:T(8,128)(2,1)} %source.2, bf16[64,64,128]{2,1,0:T(8,128)(2,1)} %field.2, f32[64,64]{1,0:T(8,128)S(1)} %copy-done.1, ...), custom_call_target="tpu_custom_call" | custom-call | flops 268435456 | bytes 6291456 | tf_op jit(solution)/shard_map/pallas_call | solution.py:19
  11.9 0.0 collective-permute-done.2.got_1
  11.9 0.0 collective-permute-done.1.got_3
  12.0 0.7 %collective-permute-done.got_2 = bf16[96,128]{1,0:T(8,128)(2,1)S(1)} collective-permute-done((bf16[96,128]{1,0:T(8,128)(2,1)S(1)}, bf16[96,128]{1,0:T(8,128)(2,1)S(1)}, u32[]{:S(2)}, u32[]{:S(2)}) %collective-permute-start) | collective-permute-done | bytes 24608 | tf_op jit(solution)/shard_map/ppermute | solution.py:375
  12.6 0.3 %shard_map.80 = (f32[2,64,128]{2,1,0:T(8,128)S(1)}, bf16[2,64,128]{2,1,0:T(8,128)(2,1)S(1)}, bf16[64,128]{1,0:T(8,128)(2,1)S(1)}, bf16[64,128]{1,0:T(8,128)(2,1)S(1)}) custom-call(bf16[96,128]{1,0:T(8,128)(2,1)S(1)} %get-tuple-element.37.far, bf16[96,128]{1,0:T(8,128)(2,1)S(1)} %get-tuple-element.38.near, bf16[96,128]{1,0:T(8,128)(2,1)S(1)} %collective-permute-done.2.got_1, ...), custom_call_target="tpu_custom_call" | custom-call | tf_op jit(solution)/shard_map/pallas_call | solution.py:19
  13.0 0.1 collective-permute-start.3
  13.1 1.6 %collective-permute-start.4 = (bf16[64,128]{1,0:T(8,128)(2,1)S(1)}, bf16[64,128]{1,0:T(8,128)(2,1)S(1)}, u32[]{:S(2)}, u32[]{:S(2)}) collective-permute-start(bf16[64,128]{1,0:T(8,128)(2,1)S(1)} %get-tuple-element.64), channel_id=1, source_target_pairs={{0,3},{1,2},{2,1},{3,0},{4,7},{5,6},{6,5},{7,4},{8,11},{9,10},{10,... | collective-permute-start | bytes 49160 | tf_op jit(solution)/shard_map/ppermute | solution.py:414
  14.7 1.4 %shard_map.81 = (bf16[64,64,128]{2,1,0:T(8,128)(2,1)}, bf16[64,64,128]{2,1,0:T(8,128)(2,1)}, f32[2,64,16,128]{3,2,1,0:T(8,128)S(1)}, bf16[32,32,128]{2,1,0:T(8,128)(2,1)S(1)}) custom-call(f32[4096,128]{1,0:T(8,128)S(1)} %get-tuple-element.49.part, f32[2,64,128]{2,1,0:T(8,128)S(1)} %get-tuple-element.54.waves, ...), custom_call_target="tpu_custom_call" | custom-call | flops 10485760 | bytes 10485760 | tf_op jit(solution)/shard_map/pallas_call | solution.py:19
  16.1 0.0 collective-permute-done.3.pair
  16.1 0.2 collective-permute-done.4.cross
  16.3 0.9 %shard_map.82 = bf16[64,64,128]{2,1,0:T(8,128)(2,1)} custom-call(f32[2,64,16,128]{3,2,1,0:T(8,128)S(1)} %get-tuple-element.61.strips, bf16[32,32,128]{2,1,0:T(8,128)(2,1)S(1)} %get-tuple-element.62.late, bf16[64,128]{1,0:T(8,128)(2,1)S(1)} %collective-permute-done.3.pair, ...), custom_call_target="tpu_custom_call", output_to_operand_aliasing={{}: (4, {})} | custom-call | tf_op jit(solution)/shard_map/pallas_call | solution.py:19
Async XLA Ops:
  0.6 9.2 %copy-start = (bf16[4,4,256,256]{3,2,1,0:T(8,128)(2,1)S(1)}, bf16[4,4,256,256]{3,2,1,0:T(8,128)(2,1)}, u32[]{:S(2)}) copy-start(bf16[4,4,256,256]{3,2,1,0:T(8,128)(2,1)} %leaf_ops.2) | copy-start | bytes 6291460
  0.6 7.9 %copy-start.1 = (f32[64,64]{1,0:T(8,128)S(1)}, f32[64,64]{1,0:T(8,128)}, u32[]{:S(2)}) copy-start(f32[64,64]{1,0:T(8,128)} %kerr.1) | copy-start | bytes 49156
  0.7 7.9 %copy-start.2 = (f32[64,64]{1,0:T(8,128)S(1)}, f32[64,64]{1,0:T(8,128)}, u32[]{:S(2)}) copy-start(f32[64,64]{1,0:T(8,128)} %wave) | copy-start | bytes 49156
  2.8 9.1 %collective-permute-start.1 = (bf16[96,128]{1,0:T(8,128)(2,1)S(1)}, bf16[96,128]{1,0:T(8,128)(2,1)S(1)}, u32[]{:S(2)}, u32[]{:S(2)}) collective-permute-start(bf16[96,128]{1,0:T(8,128)(2,1)S(1)} %get-tuple-element.37.far), channel_id=1, source_target_pairs={{0,12},{4,8},{8,4},{12,0},{1,13},{5,9},{9,5},{13,1},{2,14},{6,10},... | collective-permute-start | bytes 73736 | tf_op jit(solution)/shard_map/ppermute | solution.py:375
  7.9 4.7 %collective-permute-start = (bf16[96,128]{1,0:T(8,128)(2,1)S(1)}, bf16[96,128]{1,0:T(8,128)(2,1)S(1)}, u32[]{:S(2)}, u32[]{:S(2)}) collective-permute-start(bf16[96,128]{1,0:T(8,128)(2,1)S(1)} %get-tuple-element.37.far), channel_id=1, source_target_pairs={{0,8},{4,12},{8,0},{12,4},{1,9},{5,13},{9,1},{13,5},{2,10},{6,14},... | collective-permute-start | bytes 73736 | tf_op jit(solution)/shard_map/ppermute | solution.py:375
  7.9 4.0 %collective-permute-start.2 = (bf16[96,128]{1,0:T(8,128)(2,1)S(1)}, bf16[96,128]{1,0:T(8,128)(2,1)S(1)}, u32[]{:S(2)}, u32[]{:S(2)}) collective-permute-start(bf16[96,128]{1,0:T(8,128)(2,1)S(1)} %get-tuple-element.38.near), channel_id=1, source_target_pairs={{0,4},{4,0},{8,12},{12,8},{1,5},{5,1},{9,13},{13,9},{2,6},{6,2},{1... | collective-permute-start | bytes 73736 | tf_op jit(solution)/shard_map/ppermute | solution.py:375
  13.0 3.1 %collective-permute-start.3 = (bf16[64,128]{1,0:T(8,128)(2,1)S(1)}, bf16[64,128]{1,0:T(8,128)(2,1)S(1)}, u32[]{:S(2)}, u32[]{:S(2)}) collective-permute-start(bf16[64,128]{1,0:T(8,128)(2,1)S(1)} %get-tuple-element.63), channel_id=1, source_target_pairs={{0,1},{1,0},{2,3},{3,2},{4,5},{5,4},{6,7},{7,6},{8,9},{9,8},{10,11... | collective-permute-start | bytes 49160 | tf_op jit(solution)/shard_map/ppermute | solution.py:413
  13.1 3.2 %collective-permute-start.4 = (bf16[64,128]{1,0:T(8,128)(2,1)S(1)}, bf16[64,128]{1,0:T(8,128)(2,1)S(1)}, u32[]{:S(2)}, u32[]{:S(2)}) collective-permute-start(bf16[64,128]{1,0:T(8,128)(2,1)S(1)} %get-tuple-element.64), channel_id=1, source_target_pairs={{0,3},{1,2},{2,1},{3,0},{4,7},{5,6},{6,5},{7,4},{8,11},{9,10},{10,... | collective-permute-start | bytes 49160 | tf_op jit(solution)/shard_map/ppermute | solution.py:414

commit v5 on v4

--- a/solution.py
+++ b/solution.py
@@ -53,8 +53,8 @@
 
 
 def faces_body(
-    paired, points, parts, source, field, kerr_all, leaf_ops, transfer, far, near, edge, src, fld, ops,
-    kerr, own, kb, sems, more,
+    paired, points, parts, source, field, kerr_all, leaf_ops, transfer, far, near, edge, src, kb, fld,
+    ops, kerr, own, sems, more,
 ):
     lx, ly, pts, _ = leaf_ops.shape
     xs, ys, cols = source.shape
@@ -63,6 +63,8 @@
     size = points // parts
     coef = copy(kerr_all, kerr, more.at[0])
     coef.start()
+    matrix = copy(transfer.at[0], own, more.at[1])
+    matrix.start()
     pieces = {}
     for e, x0 in enumerate(firsts):
         for i in range(parts):
@@ -72,19 +74,22 @@
                 copy(field.at[at], fld.at[e, here], sems.at[e, 2 * i + 1]),
             )
             for c in pieces[e, i]:
-                c.start(priority=e)
+                c.start()
     rows_of = []
     for e, (a, r0) in enumerate(((0, 0), (lx - 1, pts - points))):
         rows_of.append(copy(leaf_ops.at[a, :, pl.ds(r0, points), :], ops.at[e], more.at[2 + e]))
         rows_of[e].start()
-    matrix = copy(transfer.at[0], own, more.at[1])
-    matrix.start()
     is_a, inner = seat(paired)
     coef.wait()
     kts = [kerr[x0 : x0 + points, :].T for x0 in firsts]
     for e in range(2):
         for q in range(points):
             kb[e, q] = jnp.broadcast_to(kts[e][:, q : q + 1], (ys, cols))
+    matrix.wait()
+    x_map = jnp.where(is_a, own[...], own[...].T).astype(bf16)
+    x_map = jnp.concatenate([x_map[: ys // 2], x_map[ys // 2 :]], axis=1)
+    far[ys:, :] = x_map
+    near[ys:, :] = x_map
     faces = []
     for e in range(2):
         for i in range(parts):
@@ -102,11 +107,6 @@
     toward = jnp.where(is_a, right, left)
     far[0:ys, :] = toward
     near[0:ys, :] = jnp.where(inner, jnp.where(is_a, left, right), toward)
-    matrix.wait()
-    x_map = jnp.where(is_a, own[...], own[...].T).astype(bf16)
-    x_map = jnp.concatenate([x_map[: ys // 2], x_map[ys // 2 :]], axis=1)
-    far[ys:, :] = x_map
-    near[ys:, :] = x_map
 
 
 def unpack(message):
@@ -118,46 +118,47 @@
 
 
 def leaves_body(
-    points, edge, source, field, kerr, leaf_ops, part, ends, mid, fld, rhs_all, sems
+    points, edge, source, field, kerr, wave, leaf_ops, part, ends, mid, kerr_b, wave_b,
+    fld, rhs, ops, coef, sems
 ):
     lx, ly, pts, _ = leaf_ops.shape
     xs, ys, cols = source.shape
     inner = pl.ds(points, xs - 2 * points)
-    copies = [
-        pltpu.make_async_copy(source.at[inner], mid, sems.at[0]),
-        pltpu.make_async_copy(field.at[inner], fld, sems.at[1]),
-    ]
-    for c in copies:
+    copy = pltpu.make_async_copy
+    coefs = [copy(kerr, coef.at[0], sems.at[0]), copy(wave, coef.at[1], sems.at[1])]
+    order = [0, lx - 1] + list(range(1, lx - 1))
+    middle = [copy(source.at[inner], mid, sems.at[2]), copy(field.at[inner], fld, sems.at[3])]
+    leaves = [copy(leaf_ops.at[a], ops.at[a], sems.at[4 + a]) for a in range(lx)]
+    for c in coefs + [leaves[0], leaves[lx - 1]] + middle + leaves[1 : lx - 1]:
         c.start()
 
     def leaf_row(a, rows):
+        leaves[a].wait()
         for b in range(ly):
-            rhs = rows[:, b * points : (b + 1) * points, :].reshape(pts, cols)
-            out = matmul(leaf_ops[a, b], rhs)
+            column = rows[:, b * points : (b + 1) * points, :].reshape(pts, cols)
+            out = matmul(ops[a, b], column)
             for q in range(points):
                 r = (a * points + q) * ys + b * points
                 part[r : r + points, :] = out[q * points : (q + 1) * points, :]
 
+    for c in coefs:
+        c.wait()
+    kt, wt = coef[0].T, coef[1].T
+    for x in range(xs):
+        wave_b[x] = jnp.broadcast_to(wt[:, x : x + 1], (ys, cols))
+        if points <= x < xs - points:
+            kerr_b[x - points] = jnp.broadcast_to(kt[:, x : x + 1], (ys, cols))
     leaf_row(0, edge.at[0])
     leaf_row(lx - 1, edge.at[1])
-    kt = kerr[...].T
-    for c in copies:
+    for c in middle:
         c.wait()
-    for a in range(1, lx - 1):
+    for a in order[2:]:
         for q in range(points):
-            x, r = a * points + q, (a - 1) * points + q
-            rhs_all[r] = kerr_column(mid[r], fld[r], kt[:, x : x + 1])
-        leaf_row(a, rhs_all.at[pl.ds((a - 1) * points, points)])
+            r = (a - 1) * points + q
+            rhs[r] = kerr_column(mid[r], fld[r], kerr_b[r])
+        leaf_row(a, rhs.at[pl.ds((a - 1) * points, points)])
     ends[0:xs, :] = part[pl.ds(0, xs, stride=ys), :]
     ends[xs:, :] = part[pl.ds(ys - 1, xs, stride=ys), :]
-
-
-def weights_body(kerr, wave, kerr_b, wave_b):
-    xs, ys, cols = kerr_b.shape
-    kt, wt = kerr[...].T, wave[...].T
-    for x in range(xs):
-        kerr_b[x] = jnp.broadcast_to(kt[:, x : x + 1], (ys, cols))
-        wave_b[x] = jnp.broadcast_to(wt[:, x : x + 1], (ys, cols))
 
 
 def profiles(xs):
@@ -226,16 +227,16 @@
 
 
 def update_body(
-    strip, group, chunk, last, part, waves, halo, kerr_b, wave_b, src, mid, updated, residual,
-    strips, late, u, res, sems,
+    strip, group, chunk, last, part, waves, halo, kerr_e, kerr_m, wave_b, src, mid, updated,
+    residual, strips, late, u, res, sems,
 ):
     xs, ys, cols = updated.shape
     points = src.shape[1]
 
-    def source(x):
+    def row(ends, middle, x):
         if x < points:
-            return src[0, x]
-        return src[1, x - xs + points] if x >= xs - points else mid[x - points]
+            return ends[0, x]
+        return ends[1, x - xs + points] if x >= xs - points else middle[x - points]
 
     w, z = waves[0], waves[1]
     u[0] = halo[0]
@@ -258,21 +259,22 @@
         near = matmul(taps, u[x : x + group + 2].reshape((group + 2) * ys, cols))
         for q in range(group):
             m = u[x + q + 1].astype(f32)
-            s = source(x + q).astype(f32)
-            r = near[q * ys : (q + 1) * ys] + (m * (wave_b[x + q] + kerr_b[x + q] * (m * m)) - s)
+            s = row(src, mid, x + q).astype(f32)
+            k = row(kerr_e, kerr_m, x + q)
+            r = near[q * ys : (q + 1) * ys] + (m * (wave_b[x + q] + k * (m * m)) - s)
             strips[0, x + q] = r[:strip, :]
             strips[1, x + q] = r[ys - strip :, :]
-            mid = r[strip : ys - strip, :].astype(bf16)
+            body = r[strip : ys - strip, :].astype(bf16)
             if x >= xs - last:
-                late[x + q - (xs - last)] = mid
+                late[x + q - (xs - last)] = body
             else:
-                res[x + q] = mid
+                res[x + q] = body
         end = x + group
         if end % chunk == 0 and end <= xs - last:
             at = pl.ds(end - chunk, chunk)
             send(res.at[at], residual.at[at, inside])
 
-    ahead = 64
+    ahead = xs
     rise, slope = w + z * (1.0 / xs), (z - w) * (1.0 / xs)
     for x in range(xs + ahead):
         if x < xs:
@@ -348,62 +350,57 @@
     shape = jax.ShapeDtypeStruct
     dots = 2 * lx * ly * pts * pts * cols
 
-    edges = shape((2, points, ys, cols), bf16)
-    edges = shape((2, points, ys, cols), bf16)
+    edge_shape = (2, points, ys, cols)
+    edges = shape(edge_shape, bf16)
     message = shape((ys + ys // 2, cols), bf16)
-    far, near, edge, src = call(
+    far, near, edge, src, kerr_e = call(
         functools.partial(faces_body, paired, points, 1),
-        (message, message, edges, edges),
+        (message, message, edges, edges, shape(edge_shape, f32)),
         [HBM] * 5,
         scratch=[
-            pltpu.VMEM((2, points, ys, cols), bf16),
+            pltpu.VMEM(edge_shape, bf16),
             pltpu.VMEM((2, ly, points, pts), bf16),
             pltpu.VMEM((xs, ys), f32),
             pltpu.VMEM((ys, ys), f32),
-            pltpu.VMEM((2, points, ys, cols), f32),
             pltpu.SemaphoreType.DMA((2, 2)),
             pltpu.SemaphoreType.DMA((4,)),
         ],
         cost=(dots // 8, 2 << 20),
     )(*map(in_hbm, (source, field, kerr, leaf_ops, transfer_ops)))
-    far, near, edge, source, field, kerr, wave, leaf_ops = lax.optimization_barrier(
-        (far, near, edge, source, field, kerr, wave, leaf_ops)
-    )
 
     if paired:
-        sent = [(2, far), (3, far), (1, near)]
+        sent = [(3, far), (2, far), (1, near)]
         got = [lax.ppermute(m, "gx", [(i, i ^ k) for i in range(n_gx)]) for k, m in sent]
 
-    between = shape((xs - 2 * points, ys, cols), bf16)
-    part, ends, mid = call(
+    between = (xs - 2 * points, ys, cols)
+    part, ends, mid, kerr_m, wave_b = call(
         functools.partial(leaves_body, points),
-        (shape((xs * ys, cols), f32), shape((2 * xs, cols), f32), between),
-        [VMEM, HBM, HBM, VMEM, VMEM],
+        (
+            shape((xs * ys, cols), f32),
+            shape((2 * xs, cols), f32),
+            shape(between, bf16),
+            shape(between, f32),
+            shape((xs, ys, cols), f32),
+        ),
+        [VMEM] + [HBM] * 5,
         scratch=[
-            pltpu.VMEM(between.shape, bf16),
-            pltpu.VMEM(between.shape, bf16),
-            pltpu.SemaphoreType.DMA((2,)),
+            pltpu.VMEM(between, bf16),
+            pltpu.VMEM(between, bf16),
+            pltpu.VMEM(leaf_ops.shape, bf16),
+            pltpu.VMEM((2, xs, ys), f32),
+            pltpu.SemaphoreType.DMA((4 + lx,)),
         ],
         cost=(dots, 6 << 20),
-    )(edge, in_hbm(source), in_hbm(field), kerr, leaf_ops)
-
-    kerr_b, wave_b = call(
-        weights_body,
-        (shape((xs, ys, cols), f32), shape((xs, ys, cols), f32)),
-        [VMEM] * 2,
-        cost=(xs * ys * cols, 4 << 20),
-    )(kerr, wave)
+    )(edge, *map(in_hbm, (source, field, kerr, wave, leaf_ops)))
 
     column = shape((xs, cols), bf16)
     if paired:
-        *got, part, ends, kerr_b, wave_b = lax.optimization_barrier(
-            (*got, part, ends, kerr_b, wave_b)
-        )
+        *got, part, ends = lax.optimization_barrier((*got, part, ends))
         waves, halo, pair, cross = call(
             finish_body,
             (shape((2, ys, cols), f32), shape((2, ys, cols), bf16), column, column),
             [VMEM] * 6,
-        )(far, near, got[2], got[0], got[1], ends)
+        )(far, near, got[2], got[1], got[0], ends)
     else:
         waves, halo = gathered_sweeps(far, near, ys, xs, n_gx)
         pair, cross = call(ends_body, (column, column), [VMEM] * 2)(ends, waves)
@@ -413,7 +410,7 @@
     pair = lax.ppermute(pair, "gy", pair_to)
     cross = lax.ppermute(cross, "gy", cross_to)
 
-    strip, group, chunk, last = 16, 2, xs // 4, xs // 2
+    strip, group, chunk, last = 8, 2, xs // 4, xs // 4
     big = shape((xs, ys, cols), bf16)
     updated, residual, strips, late = call(
         functools.partial(update_body, strip, group, chunk, last),
@@ -423,7 +420,7 @@
             shape((2, xs, strip, cols), f32),
             shape((last, ys - 2 * strip, cols), bf16),
         ),
-        [VMEM] * 7,
+        [VMEM] * 8,
         out_specs=(ANY, ANY, VMEM, VMEM),
         scratch=[
             pltpu.VMEM((xs + 2, ys, cols), bf16),
@@ -431,7 +428,7 @@
             pltpu.SemaphoreType.DMA((2 * xs // chunk,)),
         ],
         cost=(20 * xs * ys * cols, 10 << 20),
-    )(part, waves, halo, kerr_b, wave_b, src, mid)
+    )(part, waves, halo, kerr_e, kerr_m, wave_b, src, mid)
 
     residual = call(
         functools.partial(seam_body, n_gy, strip, last),

time: 17.3 us -> 17 us (0.983)
    pallas_call x6 -> x5, Pallas kernels: 8.15 us -> 8.02 us  [run(): pl.pallas_call(body, out_shape=outs, in_specs=ins, out_specs=out_specs if...]
  transfers between devices with their start and end apart: 5 -> 5, of which waited for: 2 -> 2; matrix products, arithmetic and copies ran while one was open for 0% -> 0% of each run, Pallas kernels for 28% -> 29%
where the time goes in v5:
time: 17 us; the launch traced here: 16.8 us
  Pallas kernels  8.02 us (47%)
  starting transfers between devices  7.36 us (43%)
  waiting for transfers between devices  0.77 us (5%)
  between operations  0.68 us (4%)
    pallas_call x5, Pallas kernels, run(): pl.pallas_call(body, out_shape=outs, in_specs=ins, out_specs=out_specs if...  8.02 us
    ppermute x3, starting transfers between devices, per_device(): lax.ppermute(m, 'gx', [(i, i ^ k) for i in range(n_gx)])  5.68 us
    ppermute x1, starting transfers between devices, per_device(): cross = lax.ppermute(cross, 'gy', cross_to)  1.61 us
    ppermute x3, waiting for transfers between devices, per_device(): lax.ppermute(m, 'gx', [(i, i ^ k) for i in range(n_gx)])  0.76 us
  transfers between devices with their start and end apart: 5, of which 2 were waited for; matrix products, arithmetic and copies ran while one was open for 0% of the time, Pallas kernels for 29%

profile of v5, /device:TPU:0, one launch (start us, length us, event | category | flops | bytes accessed | tf_op | source)
XLA Modules:
  0.0 16.8 jit_solution(9346290903726458741)
XLA Ops:
  0.6 2.0 %shard_map.77 = (bf16[96,128]{1,0:T(8,128)(2,1)S(1)}, bf16[96,128]{1,0:T(8,128)(2,1)S(1)}, bf16[2,16,64,128]{3,2,1,0:T(8,128)(2,1)S(1)}, bf16[2,16,64,128]{3,2,1,0:T(8,128)(2,1)S(1)}, f32[2,16,64,128]{3,2,1,0:T(8,128)S(1)}) custom-call(bf16[64,64,128]{2,1,0:T(8,128)(2,1)} %source.3, bf16[64,64,128]{2,1,0:T(8,128)(2,1)} %field.3, f32[64,64]{1,0:T(8,128)} %kerr.1, ...), custom_call_target="tpu_custom_call" | custom-call | flops 33554432 | bytes 2097152 | tf_op jit(solution)/shard_map/pallas_call | solution.py:19
  2.6 4.1 %collective-permute-start.1 = (bf16[96,128]{1,0:T(8,128)(2,1)S(1)}, bf16[96,128]{1,0:T(8,128)(2,1)S(1)}, u32[]{:S(2)}, u32[]{:S(2)}) collective-permute-start(bf16[96,128]{1,0:T(8,128)(2,1)S(1)} %get-tuple-element.25.far), channel_id=1, source_target_pairs={{0,8},{4,12},{8,0},{12,4},{1,9},{5,13},{9,1},{13,5},{2,10},{6,14},... | collective-permute-start | bytes 73736 | tf_op jit(solution)/shard_map/ppermute | solution.py:373
  6.7 1.3 %collective-permute-start = (bf16[96,128]{1,0:T(8,128)(2,1)S(1)}, bf16[96,128]{1,0:T(8,128)(2,1)S(1)}, u32[]{:S(2)}, u32[]{:S(2)}) collective-permute-start(bf16[96,128]{1,0:T(8,128)(2,1)S(1)} %get-tuple-element.25.far), channel_id=1, source_target_pairs={{0,12},{4,8},{8,4},{12,0},{1,13},{5,9},{9,5},{13,1},{2,14},{6,10},... | collective-permute-start | bytes 73736 | tf_op jit(solution)/shard_map/ppermute | solution.py:373
  8.1 0.2 %collective-permute-start.2 = (bf16[96,128]{1,0:T(8,128)(2,1)S(1)}, bf16[96,128]{1,0:T(8,128)(2,1)S(1)}, u32[]{:S(2)}, u32[]{:S(2)}) collective-permute-start(bf16[96,128]{1,0:T(8,128)(2,1)S(1)} %get-tuple-element.26.near), channel_id=1, source_target_pairs={{0,4},{4,0},{8,12},{12,8},{1,5},{5,1},{9,13},{13,9},{2,6},{6,2},{1... | collective-permute-start | bytes 73736 | tf_op jit(solution)/shard_map/ppermute | solution.py:373
  8.3 3.3 %shard_map.78 = (f32[4096,128]{1,0:T(8,128)S(1)}, f32[128,128]{1,0:T(8,128)S(1)}, bf16[32,64,128]{2,1,0:T(8,128)(2,1)S(1)}, f32[32,64,128]{2,1,0:T(8,128)S(1)}, f32[64,64,128]{2,1,0:T(8,128)S(1)}) custom-call(bf16[2,16,64,128]{3,2,1,0:T(8,128)(2,1)S(1)} %get-tuple-element.27.edge, bf16[64,64,128]{2,1,0:T(8,128)(2,1)} %source.3, bf16[64,64,128]{2,1,0:T(8,128)(2,1)} %field.3, ...), custom_call_target="tpu_custom_call" | custom-call | flops 268435456 | bytes 6291456 | tf_op jit(solution)/shard_map/pallas_call | solution.py:19
  11.6 0.3 %collective-permute-done.2.got_1 = bf16[96,128]{1,0:T(8,128)(2,1)S(1)} collective-permute-done((bf16[96,128]{1,0:T(8,128)(2,1)S(1)}, bf16[96,128]{1,0:T(8,128)(2,1)S(1)}, u32[]{:S(2)}, u32[]{:S(2)}) %collective-permute-start.2) | collective-permute-done | bytes 24608 | tf_op jit(solution)/shard_map/ppermute | solution.py:373
  11.9 0.0 collective-permute-done.1.got_2
  11.9 0.4 %collective-permute-done.got_3 = bf16[96,128]{1,0:T(8,128)(2,1)S(1)} collective-permute-done((bf16[96,128]{1,0:T(8,128)(2,1)S(1)}, bf16[96,128]{1,0:T(8,128)(2,1)S(1)}, u32[]{:S(2)}, u32[]{:S(2)}) %collective-permute-start) | collective-permute-done | bytes 24608 | tf_op jit(solution)/shard_map/ppermute | solution.py:373
  12.4 0.3 %shard_map.79 = (f32[2,64,128]{2,1,0:T(8,128)S(1)}, bf16[2,64,128]{2,1,0:T(8,128)(2,1)S(1)}, bf16[64,128]{1,0:T(8,128)(2,1)S(1)}, bf16[64,128]{1,0:T(8,128)(2,1)S(1)}) custom-call(bf16[96,128]{1,0:T(8,128)(2,1)S(1)} %get-tuple-element.25.far, bf16[96,128]{1,0:T(8,128)(2,1)S(1)} %get-tuple-element.26.near, bf16[96,128]{1,0:T(8,128)(2,1)S(1)} %collective-permute-done.2.got_1, ...), custom_call_target="tpu_custom_call" | custom-call | tf_op jit(solution)/shard_map/pallas_call | solution.py:19
  12.7 0.1 collective-permute-start.3
  12.8 1.6 %collective-permute-start.4 = (bf16[64,128]{1,0:T(8,128)(2,1)S(1)}, bf16[64,128]{1,0:T(8,128)(2,1)S(1)}, u32[]{:S(2)}, u32[]{:S(2)}) collective-permute-start(bf16[64,128]{1,0:T(8,128)(2,1)S(1)} %get-tuple-element.46), channel_id=1, source_target_pairs={{0,3},{1,2},{2,1},{3,0},{4,7},{5,6},{6,5},{7,4},{8,11},{9,10},{10,... | collective-permute-start | bytes 49160 | tf_op jit(solution)/shard_map/ppermute | solution.py:411
  14.4 1.6 %shard_map.80 = (bf16[64,64,128]{2,1,0:T(8,128)(2,1)}, bf16[64,64,128]{2,1,0:T(8,128)(2,1)}, f32[2,64,8,128]{3,2,1,0:T(8,128)S(1)}, bf16[16,48,128]{2,1,0:T(8,128)(2,1)S(1)}) custom-call(f32[4096,128]{1,0:T(8,128)S(1)} %get-tuple-element.30.part, f32[2,64,128]{2,1,0:T(8,128)S(1)} %get-tuple-element.35.waves, bf16[2,64,128]{2,1,0:T(8,128)(2,1)S(1)} %get-tuple-element.36.halo, ...), custom_call_target="tpu_custom_call" | custom-call | flops 10485760 | bytes 10485760 | tf_op jit(solution)/shard_map/pallas_call | solution.py:19
  16.0 0.0 collective-permute-done.3.pair
  16.0 0.0 collective-permute-done.4.cross
  16.0 0.8 %shard_map.81 = bf16[64,64,128]{2,1,0:T(8,128)(2,1)} custom-call(f32[2,64,8,128]{3,2,1,0:T(8,128)S(1)} %get-tuple-element.43.strips, bf16[16,48,128]{2,1,0:T(8,128)(2,1)S(1)} %get-tuple-element.44.late, bf16[64,128]{1,0:T(8,128)(2,1)S(1)} %collective-permute-done.3.pair, ...), custom_call_target="tpu_custom_call", output_to_operand_aliasing={{}: (4, {})} | custom-call | tf_op jit(solution)/shard_map/pallas_call | solution.py:19
Async XLA Ops:
  2.6 9.3 %collective-permute-start.1 = (bf16[96,128]{1,0:T(8,128)(2,1)S(1)}, bf16[96,128]{1,0:T(8,128)(2,1)S(1)}, u32[]{:S(2)}, u32[]{:S(2)}) collective-permute-start(bf16[96,128]{1,0:T(8,128)(2,1)S(1)} %get-tuple-element.25.far), channel_id=1, source_target_pairs={{0,8},{4,12},{8,0},{12,4},{1,9},{5,13},{9,1},{13,5},{2,10},{6,14},... | collective-permute-start | bytes 73736 | tf_op jit(solution)/shard_map/ppermute | solution.py:373
  6.7 5.6 %collective-permute-start = (bf16[96,128]{1,0:T(8,128)(2,1)S(1)}, bf16[96,128]{1,0:T(8,128)(2,1)S(1)}, u32[]{:S(2)}, u32[]{:S(2)}) collective-permute-start(bf16[96,128]{1,0:T(8,128)(2,1)S(1)} %get-tuple-element.25.far), channel_id=1, source_target_pairs={{0,12},{4,8},{8,4},{12,0},{1,13},{5,9},{9,5},{13,1},{2,14},{6,10},... | collective-permute-start | bytes 73736 | tf_op jit(solution)/shard_map/ppermute | solution.py:373
  8.1 3.8 %collective-permute-start.2 = (bf16[96,128]{1,0:T(8,128)(2,1)S(1)}, bf16[96,128]{1,0:T(8,128)(2,1)S(1)}, u32[]{:S(2)}, u32[]{:S(2)}) collective-permute-start(bf16[96,128]{1,0:T(8,128)(2,1)S(1)} %get-tuple-element.26.near), channel_id=1, source_target_pairs={{0,4},{4,0},{8,12},{12,8},{1,5},{5,1},{9,13},{13,9},{2,6},{6,2},{1... | collective-permute-start | bytes 73736 | tf_op jit(solution)/shard_map/ppermute | solution.py:373
  12.7 3.3 %collective-permute-start.3 = (bf16[64,128]{1,0:T(8,128)(2,1)S(1)}, bf16[64,128]{1,0:T(8,128)(2,1)S(1)}, u32[]{:S(2)}, u32[]{:S(2)}) collective-permute-start(bf16[64,128]{1,0:T(8,128)(2,1)S(1)} %get-tuple-element.45), channel_id=1, source_target_pairs={{0,1},{1,0},{2,3},{3,2},{4,5},{5,4},{6,7},{7,6},{8,9},{9,8},{10,11... | collective-permute-start | bytes 49160 | tf_op jit(solution)/shard_map/ppermute | solution.py:410
  12.8 3.3 %collective-permute-start.4 = (bf16[64,128]{1,0:T(8,128)(2,1)S(1)}, bf16[64,128]{1,0:T(8,128)(2,1)S(1)}, u32[]{:S(2)}, u32[]{:S(2)}) collective-permute-start(bf16[64,128]{1,0:T(8,128)(2,1)S(1)} %get-tuple-element.46), channel_id=1, source_target_pairs={{0,3},{1,2},{2,1},{3,0},{4,7},{5,6},{6,5},{7,4},{8,11},{9,10},{10,... | collective-permute-start | bytes 49160 | tf_op jit(solution)/shard_map/ppermute | solution.py:411

commit v6 on v5

--- a/solution.py
+++ b/solution.py
@@ -52,61 +52,66 @@
     return place < 2, (place == 1) | (place == 2)
 
 
-def faces_body(
-    paired, points, parts, source, field, kerr_all, leaf_ops, transfer, far, near, edge, src, kb, fld,
-    ops, kerr, own, sems, more,
+def face(points, src, fld, ops, edge, kerr_e, e):
+    ly, _, pts = ops.shape
+    cols = src.shape[2]
+    for q in range(points):
+        edge[e, q] = kerr_column(src[q], fld[q], kerr_e[e, q])
+    rows = []
+    for b in range(ly):
+        rhs = edge[e, :, b * points : (b + 1) * points, :].reshape(pts, cols)
+        rows.append(matmul(ops[b], rhs))
+    return jnp.concatenate(rows, axis=0).astype(bf16)
+
+
+def toward_body(
+    paired, points, source, field, kerr_all, leaf_ops, transfer,
+    far, edge, src, kerr_e, fld, ops, kerr, fld_1, ops_1, own, sems,
 ):
     lx, ly, pts, _ = leaf_ops.shape
     xs, ys, cols = source.shape
+    is_a, _ = seat(paired)
+    e1 = jnp.where(is_a, 1, 0)
+    e2 = 1 - e1
     copy = pltpu.make_async_copy
-    firsts = (0, xs - points)
-    size = points // parts
-    coef = copy(kerr_all, kerr, more.at[0])
-    coef.start()
-    matrix = copy(transfer.at[0], own, more.at[1])
-    matrix.start()
-    pieces = {}
-    for e, x0 in enumerate(firsts):
-        for i in range(parts):
-            at, here = pl.ds(x0 + i * size, size), pl.ds(i * size, size)
-            pieces[e, i] = (
-                copy(source.at[at], src.at[e, here], sems.at[e, 2 * i]),
-                copy(field.at[at], fld.at[e, here], sems.at[e, 2 * i + 1]),
-            )
-            for c in pieces[e, i]:
-                c.start()
-    rows_of = []
-    for e, (a, r0) in enumerate(((0, 0), (lx - 1, pts - points))):
-        rows_of.append(copy(leaf_ops.at[a, :, pl.ds(r0, points), :], ops.at[e], more.at[2 + e]))
-        rows_of[e].start()
-    is_a, inner = seat(paired)
+
+    def at_edge(e, f, o, sem):
+        x0 = pl.multiple_of(e * (xs - points), points)
+        r0 = pl.multiple_of(e * (pts - points), points)
+        return [
+            copy(source.at[pl.ds(x0, points)], src.at[e], sems.at[sem]),
+            copy(field.at[pl.ds(x0, points)], f, sems.at[sem + 1]),
+            copy(leaf_ops.at[e * (lx - 1), :, pl.ds(r0, points), :], o, sems.at[sem + 2]),
+        ]
+
+    coef = copy(kerr_all, kerr, sems.at[6])
+    matrix = copy(transfer.at[0], own, sems.at[7])
+    first = at_edge(e1, fld_1, ops_1, 0)
+    second = at_edge(e2, fld, ops, 3)
+    for c in [coef] + first + [matrix] + second:
+        c.start()
     coef.wait()
-    kts = [kerr[x0 : x0 + points, :].T for x0 in firsts]
-    for e in range(2):
+    for e, x0 in enumerate((0, xs - points)):
+        kt = kerr[x0 : x0 + points, :].T
         for q in range(points):
-            kb[e, q] = jnp.broadcast_to(kts[e][:, q : q + 1], (ys, cols))
+            kerr_e[e, q] = jnp.broadcast_to(kt[:, q : q + 1], (ys, cols))
+    for c in first:
+        c.wait()
+    far[0:ys, :] = face(points, src.at[e1], fld_1, ops_1, edge, kerr_e, e1)
     matrix.wait()
     x_map = jnp.where(is_a, own[...], own[...].T).astype(bf16)
-    x_map = jnp.concatenate([x_map[: ys // 2], x_map[ys // 2 :]], axis=1)
-    far[ys:, :] = x_map
-    near[ys:, :] = x_map
-    faces = []
-    for e in range(2):
-        for i in range(parts):
-            for c in pieces[e, i]:
-                c.wait()
-            for q in range(i * size, (i + 1) * size):
-                edge[e, q] = kerr_column(src[e, q], fld[e, q], kb[e, q])
-        rows_of[e].wait()
-        rows = []
-        for b in range(ly):
-            rhs = edge[e, :, b * points : (b + 1) * points, :].reshape(pts, cols)
-            rows.append(matmul(ops[e, b], rhs))
-        faces.append(jnp.concatenate(rows, axis=0).astype(bf16))
-    left, right = faces
-    toward = jnp.where(is_a, right, left)
-    far[0:ys, :] = toward
-    near[0:ys, :] = jnp.where(inner, jnp.where(is_a, left, right), toward)
+    far[ys:, :] = jnp.concatenate([x_map[: ys // 2], x_map[ys // 2 :]], axis=1)
+    for c in second:
+        c.wait()
+
+
+def away_body(paired, points, far, src, fld, ops, kerr_e, edge_in, near, edge):
+    ys = src.shape[2]
+    is_a, inner = seat(paired)
+    e2 = jnp.where(is_a, 0, 1)
+    other = face(points, src.at[e2], fld, ops, edge, kerr_e, e2)
+    near[0:ys, :] = jnp.where(inner, other, far[0:ys, :])
+    near[ys:, :] = far[ys:, :]
 
 
 def unpack(message):
@@ -144,18 +149,23 @@
     for c in coefs:
         c.wait()
     kt, wt = coef[0].T, coef[1].T
-    for x in range(xs):
-        wave_b[x] = jnp.broadcast_to(wt[:, x : x + 1], (ys, cols))
-        if points <= x < xs - points:
-            kerr_b[x - points] = jnp.broadcast_to(kt[:, x : x + 1], (ys, cols))
-    leaf_row(0, edge.at[0])
-    leaf_row(lx - 1, edge.at[1])
+
+    def spread(out, i, columns, x):
+        out[i] = jnp.broadcast_to(columns[:, x : x + 1], (ys, cols))
+
+    for x in range(points, xs - points):
+        spread(wave_b, x, wt, x)
+    for a, rows in ((0, edge.at[0]), (lx - 1, edge.at[1])):
+        leaf_row(a, rows)
+        for x in range(a * points, (a + 1) * points):
+            spread(wave_b, x, wt, x)
     for c in middle:
         c.wait()
     for a in order[2:]:
         for q in range(points):
-            r = (a - 1) * points + q
-            rhs[r] = kerr_column(mid[r], fld[r], kerr_b[r])
+            x, r = a * points + q, (a - 1) * points + q
+            spread(kerr_b, r, kt, x)
+            rhs[r] = kerr_column(mid[r], fld[r], kt[:, x : x + 1])
         leaf_row(a, rhs.at[pl.ds((a - 1) * points, points)])
     ends[0:xs, :] = part[pl.ds(0, xs, stride=ys), :]
     ends[xs:, :] = part[pl.ds(ys - 1, xs, stride=ys), :]
@@ -353,20 +363,29 @@
     edge_shape = (2, points, ys, cols)
     edges = shape(edge_shape, bf16)
     message = shape((ys + ys // 2, cols), bf16)
-    far, near, edge, src, kerr_e = call(
-        functools.partial(faces_body, paired, points, 1),
-        (message, message, edges, edges, shape(edge_shape, f32)),
+    rows = shape((ly, points, pts), bf16)
+    part_edge = shape(edge_shape[1:], bf16)
+    coefs = shape(edge_shape, f32)
+    far, edge, src, kerr_e, fld, ops = call(
+        functools.partial(toward_body, paired, points),
+        (message, edges, edges, coefs, part_edge, rows),
         [HBM] * 5,
         scratch=[
-            pltpu.VMEM(edge_shape, bf16),
-            pltpu.VMEM((2, ly, points, pts), bf16),
             pltpu.VMEM((xs, ys), f32),
+            pltpu.VMEM(part_edge.shape, bf16),
+            pltpu.VMEM(rows.shape, bf16),
             pltpu.VMEM((ys, ys), f32),
-            pltpu.SemaphoreType.DMA((2, 2)),
-            pltpu.SemaphoreType.DMA((4,)),
+            pltpu.SemaphoreType.DMA((8,)),
         ],
-        cost=(dots // 8, 2 << 20),
+        cost=(dots // 16, 2 << 20),
     )(*map(in_hbm, (source, field, kerr, leaf_ops, transfer_ops)))
+    near, edge = call(
+        functools.partial(away_body, paired, points),
+        (message, edges),
+        [VMEM] * 6,
+        aliases={5: 1},
+        cost=(dots // 16, 1 << 20),
+    )(far, src, fld, ops, kerr_e, edge)
 
     if paired:
         sent = [(3, far), (2, far), (1, near)]

time: 17 us -> 16.9 us (level)
  Pallas kernels: 8.02 us -> 7.6 us
  waiting for transfers between devices: 0.77 us -> 1.07 us
    pallas_call x5 -> x6, Pallas kernels: 8.02 us -> 7.6 us  [run(): pl.pallas_call(body, out_shape=outs, in_specs=ins, out_specs=out_specs if...]
    ppermute x3, waiting for transfers between devices: 0.76 us -> 1.06 us  [per_device(): lax.ppermute(m, 'gx', [(i, i ^ k) for i in range(n_gx)])]
  transfers between devices with their start and end apart: 5 -> 5, of which waited for: 2 -> 1; matrix products, arithmetic and copies ran while one was open for 0% -> 0% of each run, Pallas kernels for 29% -> 28%
where the time goes in v6:
time: 16.9 us; the launch traced here: 16.7 us
  Pallas kernels  7.6 us (45%)
  starting transfers between devices  7.37 us (44%)
  waiting for transfers between devices  1.07 us (6%)
  between operations  0.68 us (4%)
    pallas_call x6, Pallas kernels, run(): pl.pallas_call(body, out_shape=outs, in_specs=ins, out_specs=out_specs if...  7.6 us
    ppermute x3, starting transfers between devices, per_device(): lax.ppermute(m, 'gx', [(i, i ^ k) for i in range(n_gx)])  5.69 us
    ppermute x1, starting transfers between devices, per_device(): cross = lax.ppermute(cross, 'gy', cross_to)  1.61 us
    ppermute x3, waiting for transfers between devices, per_device(): lax.ppermute(m, 'gx', [(i, i ^ k) for i in range(n_gx)])  1.06 us
  transfers between devices with their start and end apart: 5, of which 1 were waited for; matrix products, arithmetic and copies ran while one was open for 0% of the time, Pallas kernels for 28%

profile of v6, /device:TPU:0, one launch (start us, length us, event | category | flops | bytes accessed | tf_op | source)
XLA Modules:
  0.0 16.7 jit_solution(10600789657132451022)
XLA Ops:
  0.6 1.8 %shard_map.77 = (bf16[96,128]{1,0:T(8,128)(2,1)S(1)}, bf16[2,16,64,128]{3,2,1,0:T(8,128)(2,1)S(1)}, bf16[2,16,64,128]{3,2,1,0:T(8,128)(2,1)S(1)}, f32[2,16,64,12...) custom-call(bf16[64,64,128]{2,1,0:T(8,128)(2,1)} %source.3, ...), custom_call_target="tpu_custom_call" | custom-call | flops 16777216 | bytes 2097152 | tf_op jit(solution)/shard_map/pallas_call | solution.py:19
  2.4 4.1 %collective-permute-start.1 = (bf16[96,128]{1,0:T(8,128)(2,1)S(1)}, bf16[96,128]{1,0:T(8,128)(2,1)S(1)}, u32[]{:S(2)}, u32[]{:S(2)}) collective-permute-start(bf16[96,128]{1,0:T(8,128)(2,1)S(1)} %get-tuple-element.28.far), channel_id=1, source_target_pairs={{0,8},{4,12},{8,0},{12,4},{1,9},{5,13},{9,1},{13,5},{2,10},{6,14},... | collective-permute-start | bytes 73736 | tf_op jit(solution)/shard_map/ppermute | solution.py:392
  6.5 1.3 %collective-permute-start = (bf16[96,128]{1,0:T(8,128)(2,1)S(1)}, bf16[96,128]{1,0:T(8,128)(2,1)S(1)}, u32[]{:S(2)}, u32[]{:S(2)}) collective-permute-start(bf16[96,128]{1,0:T(8,128)(2,1)S(1)} %get-tuple-element.28.far), channel_id=1, source_target_pairs={{0,12},{4,8},{8,4},{12,0},{1,13},{5,9},{9,5},{13,1},{2,14},{6,10},... | collective-permute-start | bytes 73736 | tf_op jit(solution)/shard_map/ppermute | solution.py:392
  7.9 0.3 %shard_map.78 = (bf16[96,128]{1,0:T(8,128)(2,1)S(1)}, bf16[2,16,64,128]{3,2,1,0:T(8,128)(2,1)S(1)}) custom-call(bf16[96,128]{1,0:T(8,128)(2,1)S(1)} %get-tuple-element.28.far, bf16[2,16,64,128]{3,2,1,0:T(8,128)(2,1)S(1)} %get-tuple-element.29.src, bf16[16,64,128]{2,1,0:T(8,128)(2,1)S(1)} %get-tuple-element.30.fld, ...), custom_call_target="tpu_custom_call", output_to_operand_aliasing={{1}: (5, {})} | custom-call | flops 16777216 | bytes 1048576 | tf_op jit(solution)/shard_map/pallas_call | solution.py:19
  8.1 0.2 %collective-permute-start.2 = (bf16[96,128]{1,0:T(8,128)(2,1)S(1)}, bf16[96,128]{1,0:T(8,128)(2,1)S(1)}, u32[]{:S(2)}, u32[]{:S(2)}) collective-permute-start(bf16[96,128]{1,0:T(8,128)(2,1)S(1)} %get-tuple-element.34.near), channel_id=1, source_target_pairs={{0,4},{4,0},{8,12},{12,8},{1,5},{5,1},{9,13},{13,9},{2,6},{6,2},{1... | collective-permute-start | bytes 73736 | tf_op jit(solution)/shard_map/ppermute | solution.py:392
  8.4 2.8 %shard_map.79 = (f32[4096,128]{1,0:T(8,128)S(1)}, f32[128,128]{1,0:T(8,128)S(1)}, bf16[32,64,128]{2,1,0:T(8,128)(2,1)S(1)}, f32[32,64,128]{2,1,0:T(8,128)S(1)}, f32[64,64,128]{2,1,0:T(8,128)S(1)}) custom-call(bf16[2,16,64,128]{3,2,1,0:T(8,128)(2,1)S(1)} %get-tuple-element.35.edge, bf16[64,64,128]{2,1,0:T(8,128)(2,1)} %source.3, bf16[64,64,128]{2,1,0:T(8,128)(2,1)} %field.3, ...), custom_call_target="tpu_custom_call" | custom-call | flops 268435456 | bytes 6291456 | tf_op jit(solution)/shard_map/pallas_call | solution.py:19
  11.2 1.1 %collective-permute-done.2.got_1 = bf16[96,128]{1,0:T(8,128)(2,1)S(1)} collective-permute-done((bf16[96,128]{1,0:T(8,128)(2,1)S(1)}, bf16[96,128]{1,0:T(8,128)(2,1)S(1)}, u32[]{:S(2)}, u32[]{:S(2)}) %collective-permute-start.2) | collective-permute-done | bytes 24608 | tf_op jit(solution)/shard_map/ppermute | solution.py:392
  12.2 0.0 collective-permute-done.1.got_2
  12.2 0.0 collective-permute-done.got_3
  12.2 0.3 %shard_map.80 = (f32[2,64,128]{2,1,0:T(8,128)S(1)}, bf16[2,64,128]{2,1,0:T(8,128)(2,1)S(1)}, bf16[64,128]{1,0:T(8,128)(2,1)S(1)}, bf16[64,128]{1,0:T(8,128)(2,1)S(1)}) custom-call(bf16[96,128]{1,0:T(8,128)(2,1)S(1)} %get-tuple-element.28.far, bf16[96,128]{1,0:T(8,128)(2,1)S(1)} %get-tuple-element.34.near, bf16[96,128]{1,0:T(8,128)(2,1)S(1)} %collective-permute-done.2.got_1, ...), custom_call_target="tpu_custom_call" | custom-call | tf_op jit(solution)/shard_map/pallas_call | solution.py:19
  12.6 0.1 collective-permute-start.3
  12.7 1.6 %collective-permute-start.4 = (bf16[64,128]{1,0:T(8,128)(2,1)S(1)}, bf16[64,128]{1,0:T(8,128)(2,1)S(1)}, u32[]{:S(2)}, u32[]{:S(2)}) collective-permute-start(bf16[64,128]{1,0:T(8,128)(2,1)S(1)} %get-tuple-element.52), channel_id=1, source_target_pairs={{0,3},{1,2},{2,1},{3,0},{4,7},{5,6},{6,5},{7,4},{8,11},{9,10},{10,... | collective-permute-start | bytes 49160 | tf_op jit(solution)/shard_map/ppermute | solution.py:430
  14.3 1.6 %shard_map.81 = (bf16[64,64,128]{2,1,0:T(8,128)(2,1)}, bf16[64,64,128]{2,1,0:T(8,128)(2,1)}, f32[2,64,8,128]{3,2,1,0:T(8,128)S(1)}, bf16[16,48,128]{2,1,0:T(8,128)(2,1)S(1)}) custom-call(f32[4096,128]{1,0:T(8,128)S(1)} %get-tuple-element.38.part, f32[2,64,128]{2,1,0:T(8,128)S(1)} %get-tuple-element.43.waves, bf16[2,64,128]{2,1,0:T(8,128)(2,1)S(1)} %get-tuple-element.44.halo, ...), custom_call_target="tpu_custom_call" | custom-call | flops 10485760 | bytes 10485760 | tf_op jit(solution)/shard_map/pallas_call | solution.py:19
  15.9 0.0 collective-permute-done.3.pair
  15.9 0.0 collective-permute-done.4.cross
  15.9 0.8 %shard_map.82 = bf16[64,64,128]{2,1,0:T(8,128)(2,1)} custom-call(f32[2,64,8,128]{3,2,1,0:T(8,128)S(1)} %get-tuple-element.49.strips, bf16[16,48,128]{2,1,0:T(8,128)(2,1)S(1)} %get-tuple-element.50.late, bf16[64,128]{1,0:T(8,128)(2,1)S(1)} %collective-permute-done.3.pair, ...), custom_call_target="tpu_custom_call", output_to_operand_aliasing={{}: (4, {})} | custom-call | tf_op jit(solution)/shard_map/pallas_call | solution.py:19
Async XLA Ops:
  2.4 9.8 %collective-permute-start.1 = (bf16[96,128]{1,0:T(8,128)(2,1)S(1)}, bf16[96,128]{1,0:T(8,128)(2,1)S(1)}, u32[]{:S(2)}, u32[]{:S(2)}) collective-permute-start(bf16[96,128]{1,0:T(8,128)(2,1)S(1)} %get-tuple-element.28.far), channel_id=1, source_target_pairs={{0,8},{4,12},{8,0},{12,4},{1,9},{5,13},{9,1},{13,5},{2,10},{6,14},... | collective-permute-start | bytes 73736 | tf_op jit(solution)/shard_map/ppermute | solution.py:392
  6.5 5.7 %collective-permute-start = (bf16[96,128]{1,0:T(8,128)(2,1)S(1)}, bf16[96,128]{1,0:T(8,128)(2,1)S(1)}, u32[]{:S(2)}, u32[]{:S(2)}) collective-permute-start(bf16[96,128]{1,0:T(8,128)(2,1)S(1)} %get-tuple-element.28.far), channel_id=1, source_target_pairs={{0,12},{4,8},{8,4},{12,0},{1,13},{5,9},{9,5},{13,1},{2,14},{6,10},... | collective-permute-start | bytes 73736 | tf_op jit(solution)/shard_map/ppermute | solution.py:392
  8.1 4.1 %collective-permute-start.2 = (bf16[96,128]{1,0:T(8,128)(2,1)S(1)}, bf16[96,128]{1,0:T(8,128)(2,1)S(1)}, u32[]{:S(2)}, u32[]{:S(2)}) collective-permute-start(bf16[96,128]{1,0:T(8,128)(2,1)S(1)} %get-tuple-element.34.near), channel_id=1, source_target_pairs={{0,4},{4,0},{8,12},{12,8},{1,5},{5,1},{9,13},{13,9},{2,6},{6,2},{1... | collective-permute-start | bytes 73736 | tf_op jit(solution)/shard_map/ppermute | solution.py:392
  12.6 3.3 %collective-permute-start.3 = (bf16[64,128]{1,0:T(8,128)(2,1)S(1)}, bf16[64,128]{1,0:T(8,128)(2,1)S(1)}, u32[]{:S(2)}, u32[]{:S(2)}) collective-permute-start(bf16[64,128]{1,0:T(8,128)(2,1)S(1)} %get-tuple-element.51), channel_id=1, source_target_pairs={{0,1},{1,0},{2,3},{3,2},{4,5},{5,4},{6,7},{7,6},{8,9},{9,8},{10,11... | collective-permute-start | bytes 49160 | tf_op jit(solution)/shard_map/ppermute | solution.py:429
  12.7 3.3 %collective-permute-start.4 = (bf16[64,128]{1,0:T(8,128)(2,1)S(1)}, bf16[64,128]{1,0:T(8,128)(2,1)S(1)}, u32[]{:S(2)}, u32[]{:S(2)}) collective-permute-start(bf16[64,128]{1,0:T(8,128)(2,1)S(1)} %get-tuple-element.52), channel_id=1, source_target_pairs={{0,3},{1,2},{2,1},{3,0},{4,7},{5,6},{6,5},{7,4},{8,11},{9,10},{10,... | collective-permute-start | bytes 49160 | tf_op jit(solution)/shard_map/ppermute | solution.py:430

commit v7 on v6

--- a/solution.py
+++ b/solution.py
@@ -52,11 +52,12 @@
     return place < 2, (place == 1) | (place == 2)
 
 
-def face(points, src, fld, ops, edge, kerr_e, e):
+def face(points, src, fld, ops, coef, edge, kerr_e, e):
     ly, _, pts = ops.shape
     cols = src.shape[2]
     for q in range(points):
-        edge[e, q] = kerr_column(src[q], fld[q], kerr_e[e, q])
+        kerr_e[e, q] = jnp.broadcast_to(coef[:, q : q + 1], src.shape[1:])
+        edge[e, q] = kerr_column(src[q], fld[q], coef[:, q : q + 1])
     rows = []
     for b in range(ly):
         rhs = edge[e, :, b * points : (b + 1) * points, :].reshape(pts, cols)
@@ -91,13 +92,10 @@
     for c in [coef] + first + [matrix] + second:
         c.start()
     coef.wait()
-    for e, x0 in enumerate((0, xs - points)):
-        kt = kerr[x0 : x0 + points, :].T
-        for q in range(points):
-            kerr_e[e, q] = jnp.broadcast_to(kt[:, q : q + 1], (ys, cols))
+    kt = kerr[pl.ds(pl.multiple_of(e1 * (xs - points), points), points), :].T
     for c in first:
         c.wait()
-    far[0:ys, :] = face(points, src.at[e1], fld_1, ops_1, edge, kerr_e, e1)
+    far[0:ys, :] = face(points, src.at[e1], fld_1, ops_1, kt, edge, kerr_e, e1)
     matrix.wait()
     x_map = jnp.where(is_a, own[...], own[...].T).astype(bf16)
     far[ys:, :] = jnp.concatenate([x_map[: ys // 2], x_map[ys // 2 :]], axis=1)
@@ -105,11 +103,12 @@
         c.wait()
 
 
-def away_body(paired, points, far, src, fld, ops, kerr_e, edge_in, near, edge):
-    ys = src.shape[2]
+def away_body(paired, points, far, src, fld, ops, kerr, edge_in, kerr_in, near, edge, kerr_e):
+    xs, ys = kerr.shape
     is_a, inner = seat(paired)
     e2 = jnp.where(is_a, 0, 1)
-    other = face(points, src.at[e2], fld, ops, edge, kerr_e, e2)
+    kt = kerr[pl.ds(pl.multiple_of(e2 * (xs - points), points), points), :].T
+    other = face(points, src.at[e2], fld, ops, kt, edge, kerr_e, e2)
     near[0:ys, :] = jnp.where(inner, other, far[0:ys, :])
     near[ys:, :] = far[ys:, :]
 
@@ -190,22 +189,17 @@
 def finish_body(far, near, got_1, got_2, got_3, ends, waves, halo, pair, cross):
     xs = pair.shape[0]
     is_a, inner = seat(True)
-    own_face, own_map = unpack(far[...])
-    own_near, _ = unpack(near[...])
-    mate_face, mate_map = unpack(got_1[...])
-    face_2, map_2 = unpack(got_2[...])
-    face_3, map_3 = unpack(got_3[...])
-    other_map = jnp.where(inner, map_3, map_2)
-    other_in = jnp.where(inner, face_3, face_2).astype(f32)
-    other_out = jnp.where(inner, face_2, face_3)
+    ys = got_1.shape[0] * 2 // 3
+    mine, mate, second, third = far[...], got_1[...], got_2[...], got_3[...]
+    other_in, other_map = unpack(jnp.where(inner, third, second))
+    other_out = jnp.where(inner, second[:ys], third[:ys])
+    other_in = other_in.astype(f32)
     back_in = matmul(other_map, other_out) + other_in
-    in_map = jnp.where(inner, own_map, mate_map)
-    out_face = jnp.where(inner, mate_face, own_face)
-    in_back = jnp.where(inner, own_near, mate_face).astype(f32)
-    reach = matmul(in_map, out_face) + own_face.astype(f32)
-    back_out = in_back + lax.dot_general(
-        in_map, back_in.astype(bf16), (((0,), (0,)), ((), ())), preferred_element_type=f32
-    )
+    _, in_map = unpack(jnp.where(inner, mine, mate))
+    out_face = jnp.where(inner, mate[:ys], mine[:ys])
+    in_back = jnp.where(inner, near[0:ys, :], mate[:ys]).astype(f32)
+    reach = matmul(in_map, out_face) + mine[:ys].astype(f32)
+    back_out = in_back + matmul(in_map.astype(f32).T.astype(bf16), back_in.astype(bf16))
     out_face, other_out = out_face.astype(f32), other_out.astype(f32)
     ahead = jnp.where(inner, out_face, 0.0)
     back = jnp.where(inner, back_in, back_out)
@@ -366,12 +360,11 @@
     rows = shape((ly, points, pts), bf16)
     part_edge = shape(edge_shape[1:], bf16)
     coefs = shape(edge_shape, f32)
-    far, edge, src, kerr_e, fld, ops = call(
+    far, edge, src, kerr_e, fld, ops, kerr_v = call(
         functools.partial(toward_body, paired, points),
-        (message, edges, edges, coefs, part_edge, rows),
+        (message, edges, edges, coefs, part_edge, rows, shape((xs, ys), f32)),
         [HBM] * 5,
         scratch=[
-            pltpu.VMEM((xs, ys), f32),
             pltpu.VMEM(part_edge.shape, bf16),
             pltpu.VMEM(rows.shape, bf16),
             pltpu.VMEM((ys, ys), f32),
@@ -379,16 +372,16 @@
         ],
         cost=(dots // 16, 2 << 20),
     )(*map(in_hbm, (source, field, kerr, leaf_ops, transfer_ops)))
-    near, edge = call(
+    near, edge, kerr_e = call(
         functools.partial(away_body, paired, points),
-        (message, edges),
-        [VMEM] * 6,
-        aliases={5: 1},
+        (message, edges, coefs),
+        [VMEM] * 7,
+        aliases={5: 1, 6: 2},
         cost=(dots // 16, 1 << 20),
-    )(far, src, fld, ops, kerr_e, edge)
+    )(far, src, fld, ops, kerr_v, edge, kerr_e)
 
     if paired:
-        sent = [(3, far), (2, far), (1, near)]
+        sent = [(2, far), (3, far), (1, near)]
         got = [lax.ppermute(m, "gx", [(i, i ^ k) for i in range(n_gx)]) for k, m in sent]
 
     between = (xs - 2 * points, ys, cols)
@@ -419,7 +412,7 @@
             finish_body,
             (shape((2, ys, cols), f32), shape((2, ys, cols), bf16), column, column),
             [VMEM] * 6,
-        )(far, near, got[2], got[1], got[0], ends)
+        )(far, near, got[2], got[0], got[1], ends)
     else:
         waves, halo = gathered_sweeps(far, near, ys, xs, n_gx)
         pair, cross = call(ends_body, (column, column), [VMEM] * 2)(ends, waves)

time: 16.9 us -> 16.8 us (level)
  waiting for transfers between devices: 1.07 us -> 0.78 us
    ppermute x3, waiting for transfers between devices: 1.06 us -> 0.77 us  [per_device(): lax.ppermute(m, 'gx', [(i, i ^ k) for i in range(n_gx)])]
  transfers between devices with their start and end apart: 5 -> 5, of which waited for: 1 -> 2; matrix products, arithmetic and copies ran while one was open for 0% -> 0% of each run, Pallas kernels for 28% -> 29%
where the time goes in v7:
time: 16.8 us; the launch traced here: 16.7 us
  Pallas kernels  7.74 us (46%)
  starting transfers between devices  7.45 us (44%)
  waiting for transfers between devices  0.78 us (5%)
  between operations  0.69 us (4%)
    pallas_call x6, Pallas kernels, run(): pl.pallas_call(body, out_shape=outs, in_specs=ins, out_specs=out_specs if...  7.74 us
    ppermute x3, starting transfers between devices, per_device(): lax.ppermute(m, 'gx', [(i, i ^ k) for i in range(n_gx)])  5.77 us
    ppermute x1, starting transfers between devices, per_device(): cross = lax.ppermute(cross, 'gy', cross_to)  1.61 us
    ppermute x3, waiting for transfers between devices, per_device(): lax.ppermute(m, 'gx', [(i, i ^ k) for i in range(n_gx)])  0.77 us
  transfers between devices with their start and end apart: 5, of which 2 were waited for; matrix products, arithmetic and copies ran while one was open for 0% of the time, Pallas kernels for 29%

profile of v7, /device:TPU:0, one launch (start us, length us, event | category | flops | bytes accessed | tf_op | source)
XLA Modules:
  0.0 16.7 jit_solution(6277697919079845725)
XLA Ops:
  0.6 1.7 %shard_map.77 = (bf16[96,128]{1,0:T(8,128)(2,1)S(1)}, bf16[2,16,64,128]{3,2,1,0:T(8,128)(2,1)S(1)}, bf16[2,16,64,128]{3,2,1,0:T(8,128)(2,1)S(1)}, f32[2,16,64,12...) custom-call(bf16[64,64,128]{2,1,0:T(8,128)(2,1)} %source.3, ...), custom_call_target="tpu_custom_call" | custom-call | flops 16777216 | bytes 2097152 | tf_op jit(solution)/shard_map/pallas_call | solution.py:19
  2.3 5.1 %collective-permute-start.1 = (bf16[96,128]{1,0:T(8,128)(2,1)S(1)}, bf16[96,128]{1,0:T(8,128)(2,1)S(1)}, u32[]{:S(2)}, u32[]{:S(2)}) collective-permute-start(bf16[96,128]{1,0:T(8,128)(2,1)S(1)} %get-tuple-element.30.far), channel_id=1, source_target_pairs={{0,12},{4,8},{8,4},{12,0},{1,13},{5,9},{9,5},{13,1},{2,14},{6,10},... | collective-permute-start | bytes 73736 | tf_op jit(solution)/shard_map/ppermute | solution.py:385
  7.4 0.0 collective-permute-start
  7.4 0.5 %shard_map.78 = (bf16[96,128]{1,0:T(8,128)(2,1)S(1)}, bf16[2,16,64,128]{3,2,1,0:T(8,128)(2,1)S(1)}, f32[2,16,64,128]{3,2,1,0:T(8,128)S(1)}) custom-call(bf16[96,128]{1,0:T(8,128)(2,1)S(1)} %get-tuple-element.30.far, bf16[2,16,64,128]{3,2,1,0:T(8,128)(2,1)S(1)} %get-tuple-element.31.src, ...), custom_call_target="tpu_custom_call", output_to_operand_aliasing={{1}: (5, {}), {2}: (6, {})} | custom-call | flops 16777216 | bytes 1048576 | tf_op jit(solution)/shard_map/pallas_call | solution.py:19
  8.0 0.7 %collective-permute-start.2 = (bf16[96,128]{1,0:T(8,128)(2,1)S(1)}, bf16[96,128]{1,0:T(8,128)(2,1)S(1)}, u32[]{:S(2)}, u32[]{:S(2)}) collective-permute-start(bf16[96,128]{1,0:T(8,128)(2,1)S(1)} %get-tuple-element.37.near), channel_id=1, source_target_pairs={{0,4},{4,0},{8,12},{12,8},{1,5},{5,1},{9,13},{13,9},{2,6},{6,2},{1... | collective-permute-start | bytes 73736 | tf_op jit(solution)/shard_map/ppermute | solution.py:385
  8.6 2.8 %shard_map.79 = (f32[4096,128]{1,0:T(8,128)S(1)}, f32[128,128]{1,0:T(8,128)S(1)}, bf16[32,64,128]{2,1,0:T(8,128)(2,1)S(1)}, f32[32,64,128]{2,1,0:T(8,128)S(1)}, f32[64,64,128]{2,1,0:T(8,128)S(1)}) custom-call(bf16[2,16,64,128]{3,2,1,0:T(8,128)(2,1)S(1)} %get-tuple-element.38.edge, bf16[64,64,128]{2,1,0:T(8,128)(2,1)} %source.3, bf16[64,64,128]{2,1,0:T(8,128)(2,1)} %field.3, ...), custom_call_target="tpu_custom_call" | custom-call | flops 268435456 | bytes 6291456 | tf_op jit(solution)/shard_map/pallas_call | solution.py:19
  11.4 0.4 %collective-permute-done.2.got_1 = bf16[96,128]{1,0:T(8,128)(2,1)S(1)} collective-permute-done((bf16[96,128]{1,0:T(8,128)(2,1)S(1)}, bf16[96,128]{1,0:T(8,128)(2,1)S(1)}, u32[]{:S(2)}, u32[]{:S(2)}) %collective-permute-start.2) | collective-permute-done | bytes 24608 | tf_op jit(solution)/shard_map/ppermute | solution.py:385
  11.8 0.0 collective-permute-done.1.got_3
  11.8 0.4 %collective-permute-done.got_2 = bf16[96,128]{1,0:T(8,128)(2,1)S(1)} collective-permute-done((bf16[96,128]{1,0:T(8,128)(2,1)S(1)}, bf16[96,128]{1,0:T(8,128)(2,1)S(1)}, u32[]{:S(2)}, u32[]{:S(2)}) %collective-permute-start) | collective-permute-done | bytes 24608 | tf_op jit(solution)/shard_map/ppermute | solution.py:385
  12.2 0.3 %shard_map.80 = (f32[2,64,128]{2,1,0:T(8,128)S(1)}, bf16[2,64,128]{2,1,0:T(8,128)(2,1)S(1)}, bf16[64,128]{1,0:T(8,128)(2,1)S(1)}, bf16[64,128]{1,0:T(8,128)(2,1)S(1)}) custom-call(bf16[96,128]{1,0:T(8,128)(2,1)S(1)} %get-tuple-element.30.far, bf16[96,128]{1,0:T(8,128)(2,1)S(1)} %get-tuple-element.37.near, bf16[96,128]{1,0:T(8,128)(2,1)S(1)} %collective-permute-done.2.got_1, ...), custom_call_target="tpu_custom_call" | custom-call | tf_op jit(solution)/shard_map/pallas_call | solution.py:19
  12.5 0.1 collective-permute-start.3
  12.6 1.6 %collective-permute-start.4 = (bf16[64,128]{1,0:T(8,128)(2,1)S(1)}, bf16[64,128]{1,0:T(8,128)(2,1)S(1)}, u32[]{:S(2)}, u32[]{:S(2)}) collective-permute-start(bf16[64,128]{1,0:T(8,128)(2,1)S(1)} %get-tuple-element.56), channel_id=1, source_target_pairs={{0,3},{1,2},{2,1},{3,0},{4,7},{5,6},{6,5},{7,4},{8,11},{9,10},{10,... | collective-permute-start | bytes 49160 | tf_op jit(solution)/shard_map/ppermute | solution.py:423
  14.2 1.6 %shard_map.81 = (bf16[64,64,128]{2,1,0:T(8,128)(2,1)}, bf16[64,64,128]{2,1,0:T(8,128)(2,1)}, f32[2,64,8,128]{3,2,1,0:T(8,128)S(1)}, bf16[16,48,128]{2,1,0:T(8,128)(2,1)S(1)}) custom-call(f32[4096,128]{1,0:T(8,128)S(1)} %get-tuple-element.41.part, f32[2,64,128]{2,1,0:T(8,128)S(1)} %get-tuple-element.46.waves, bf16[2,64,128]{2,1,0:T(8,128)(2,1)S(1)} %get-tuple-element.47.halo, ...), custom_call_target="tpu_custom_call" | custom-call | flops 10485760 | bytes 10485760 | tf_op jit(solution)/shard_map/pallas_call | solution.py:19
  15.8 0.0 collective-permute-done.3.pair
  15.9 0.0 collective-permute-done.4.cross
  15.9 0.8 %shard_map.82 = bf16[64,64,128]{2,1,0:T(8,128)(2,1)} custom-call(f32[2,64,8,128]{3,2,1,0:T(8,128)S(1)} %get-tuple-element.53.strips, bf16[16,48,128]{2,1,0:T(8,128)(2,1)S(1)} %get-tuple-element.54.late, bf16[64,128]{1,0:T(8,128)(2,1)S(1)} %collective-permute-done.3.pair, ...), custom_call_target="tpu_custom_call", output_to_operand_aliasing={{}: (4, {})} | custom-call | tf_op jit(solution)/shard_map/pallas_call | solution.py:19
Async XLA Ops:
  2.3 9.5 %collective-permute-start.1 = (bf16[96,128]{1,0:T(8,128)(2,1)S(1)}, bf16[96,128]{1,0:T(8,128)(2,1)S(1)}, u32[]{:S(2)}, u32[]{:S(2)}) collective-permute-start(bf16[96,128]{1,0:T(8,128)(2,1)S(1)} %get-tuple-element.30.far), channel_id=1, source_target_pairs={{0,12},{4,8},{8,4},{12,0},{1,13},{5,9},{9,5},{13,1},{2,14},{6,10},... | collective-permute-start | bytes 73736 | tf_op jit(solution)/shard_map/ppermute | solution.py:385
  7.4 4.7 %collective-permute-start = (bf16[96,128]{1,0:T(8,128)(2,1)S(1)}, bf16[96,128]{1,0:T(8,128)(2,1)S(1)}, u32[]{:S(2)}, u32[]{:S(2)}) collective-permute-start(bf16[96,128]{1,0:T(8,128)(2,1)S(1)} %get-tuple-element.30.far), channel_id=1, source_target_pairs={{0,8},{4,12},{8,0},{12,4},{1,9},{5,13},{9,1},{13,5},{2,10},{6,14},... | collective-permute-start | bytes 73736 | tf_op jit(solution)/shard_map/ppermute | solution.py:385
  8.0 3.8 %collective-permute-start.2 = (bf16[96,128]{1,0:T(8,128)(2,1)S(1)}, bf16[96,128]{1,0:T(8,128)(2,1)S(1)}, u32[]{:S(2)}, u32[]{:S(2)}) collective-permute-start(bf16[96,128]{1,0:T(8,128)(2,1)S(1)} %get-tuple-element.37.near), channel_id=1, source_target_pairs={{0,4},{4,0},{8,12},{12,8},{1,5},{5,1},{9,13},{13,9},{2,6},{6,2},{1... | collective-permute-start | bytes 73736 | tf_op jit(solution)/shard_map/ppermute | solution.py:385
  12.5 3.3 %collective-permute-start.3 = (bf16[64,128]{1,0:T(8,128)(2,1)S(1)}, bf16[64,128]{1,0:T(8,128)(2,1)S(1)}, u32[]{:S(2)}, u32[]{:S(2)}) collective-permute-start(bf16[64,128]{1,0:T(8,128)(2,1)S(1)} %get-tuple-element.55), channel_id=1, source_target_pairs={{0,1},{1,0},{2,3},{3,2},{4,5},{5,4},{6,7},{7,6},{8,9},{9,8},{10,11... | collective-permute-start | bytes 49160 | tf_op jit(solution)/shard_map/ppermute | solution.py:422
  12.6 3.3 %collective-permute-start.4 = (bf16[64,128]{1,0:T(8,128)(2,1)S(1)}, bf16[64,128]{1,0:T(8,128)(2,1)S(1)}, u32[]{:S(2)}, u32[]{:S(2)}) collective-permute-start(bf16[64,128]{1,0:T(8,128)(2,1)S(1)} %get-tuple-element.56), channel_id=1, source_target_pairs={{0,3},{1,2},{2,1},{3,0},{4,7},{5,6},{6,5},{7,4},{8,11},{9,10},{10,... | collective-permute-start | bytes 49160 | tf_op jit(solution)/shard_map/ppermute | solution.py:423
